TPU v7x, 32 devices: a whole 2x2x4 slice. The times are simulated.
32 devices in a mesh: groups: 2 (over x), expert: 8 (over z, y), sub: 2 (over core).
Axes of the slice: x: 2, y: 2, z: 4, core: 2. Of those that a mesh axis runs over, the one named last changes fastest.
Arguments:
- hidden_state: bfloat16 [2048, 2048], P(('groups', 'expert', 'sub')), parts along dimension 0, may hold values from -6 to 6
- norm_gain: float32 [2048], replicated, may hold values from 0.5 to 1.5
- router_weight: bfloat16 [2048, 16], replicated, may hold values from -0.25 to 0.25
- expert_ids: int32 [2048, 6], P(('groups', 'expert', 'sub')), parts along dimension 0, may hold values from 0 to 15, all different within a row; in each aligned block of 64 rows (0 to 63, 64 to 127, ...) at most 32 rows name the same one
- live_counts: int32 [32], P(('groups', 'expert', 'sub')), parts along dimension 0, may hold values from 16 to 64
- routed_gate_up: bfloat16 [16, 2048, 2816], P(('expert', 'sub')), may hold values from -0.125 to 0.125
- routed_down: bfloat16 [16, 1408, 2048], P(('expert', 'sub')), may hold values from -0.15625 to 0.15625
- shared_weights: bfloat16 [3, 2048, 2816], P(None, None, 'expert'), may hold values from -0.125 to 0.125
Outputs:
- mixed: bfloat16 [2048, 2048], P(('groups', 'expert', 'sub')), parts along dimension 0
- penalty: float32 [2], P('groups'), parts along dimension 0
There are 2 independent parts, one for each index of `groups`. A program takes and returns all parts, laid end to end along the dimension named above; an argument that names none is the same for every part. Nothing has to cross between parts.
Inputs may be any that keep to these rules, and one draw needn't show every extreme that they name: `expert_ids`: in each row the 6 experts differ; among the 64 rows of one device no expert is named more than 32 times.
All inputs are finite; a program needn't handle non-finite values.
Results may differ from a plain program's by a relative error of at most 0.0065.
Values may be sent and summed in bfloat16 or wider, within the bound.
No kernel may reach another device: no remote copies, remote signals or barrier semaphores. Data moves between devices by JAX's collectives and lax.ppermute only.
A program may use at most 128 MiB of HBM per device.

v0:
```python
import functools

import jax
import jax.numpy as jnp
from jax import lax
from jax.experimental import pallas as pl
from jax.experimental.pallas import tpu as pltpu
from jax.sharding import PartitionSpec as P


F32 = jnp.float32
BF16 = jnp.bfloat16
VMEM = pl.BlockSpec(memory_space=pltpu.VMEM)
SMEM = pl.BlockSpec(memory_space=pltpu.SMEM)
ANY = pl.BlockSpec(memory_space=pl.ANY)


def split_three(values):
    high = values.astype(BF16)
    rest = values - high.astype(F32)
    middle = rest.astype(BF16)
    low = (rest - middle.astype(F32)).astype(BF16)
    return high, middle, low


def iota(shape, axis):
    return lax.broadcasted_iota(jnp.int32, shape, axis)


def my_seat():
    me = lax.axis_index("expert") * 2 + lax.axis_index("sub")
    return me, me ^ 1


def route_kernel(live_ref, hidden_ref, gain_ref, router_ref, ids_ref, packet_ref):
    rows, width = hidden_ref.shape
    experts = router_ref.shape[0]
    lanes = packet_ref.shape[1] - width
    values = hidden_ref[...].astype(F32)
    spread = jnp.mean(values * values, axis=-1, keepdims=True)
    normed = (values * lax.rsqrt(spread + 1e-06) * gain_ref[...]).astype(BF16)
    packet_ref[:, :width] = normed
    logits = lax.dot_general(
        router_ref[...], normed, (((1,), (1,)), ((), ())), preferred_element_type=F32
    )
    probs = 1.0 / (1.0 + jnp.exp(-logits))
    live = (iota((1, rows), 1) < live_ref[0]).astype(F32)
    seats = iota((experts, rows), 0)
    named = jnp.zeros((experts, rows), F32)
    for k in range(ids_ref.shape[0]):
        named = named + (ids_ref[k : k + 1, :] == seats).astype(F32)
    picked = named * probs
    weights = (live * picked / jnp.sum(picked, axis=0, keepdims=True)).astype(BF16)
    taken = named * live
    earlier = (iota((rows, rows), 0) < iota((rows, rows), 1)).astype(F32).astype(BF16)
    slot = jnp.dot(taken.astype(BF16), earlier, preferred_element_type=F32)
    code = (taken * (slot + 1.0)).astype(BF16)
    load = jnp.sum(taken, axis=1, keepdims=True).astype(BF16)
    mass = jnp.sum(probs * live, axis=1, keepdims=True)
    meta = jnp.zeros((rows, lanes), F32)
    for at, piece in enumerate([weights, code, load, *split_three(mass)]):
        put = iota((experts, lanes), 1) == iota((experts, lanes), 0) + at * experts
        piece = jnp.broadcast_to(piece.astype(F32), (experts, rows)).astype(BF16)
        meta = meta + lax.dot_general(
            piece,
            put.astype(F32).astype(BF16),
            (((0,), (0,)), ((), ())),
            preferred_element_type=F32,
        )
    packet_ref[:, width:] = meta.astype(BF16)


def columns_of(block_ref, width, at):
    notes = block_ref[:, width:].astype(F32)
    lane = iota(notes.shape, 1)
    return [jnp.sum(jnp.where(lane == a, notes, 0.0), axis=1, keepdims=True) for a in at]


def matches(block_ref, width, experts, capacity):
    me, peer = my_seat()
    rows = block_ref.shape[0]
    mine, theirs = columns_of(block_ref, width, [experts + me, experts + peer])
    slot = iota((rows, 2 * capacity), 1)
    place = jnp.where(slot < capacity, mine, theirs).astype(jnp.int32)
    return (place - 1) == jnp.where(slot < capacity, slot, slot - capacity), slot


def pick_kernel(count, width, experts, capacity, *refs):
    blocks, (mine_ref, peer_ref) = refs[:count], refs[count:]
    sums = []
    for i, block in enumerate(blocks):
        match, _ = matches(block, width, experts, capacity)
        rows = lax.dot_general(
            match.astype(F32).astype(BF16),
            block[:, :width],
            (((0,), (0,)), ((), ())),
            preferred_element_type=F32,
        ).astype(BF16)
        mine_ref[i * capacity : (i + 1) * capacity, :] = rows[:capacity]
        peer_ref[i * capacity : (i + 1) * capacity, :] = rows[capacity:]
        sums.append(block[0:1, width:].astype(F32))
    filler = jnp.zeros((16 - count, sums[0].shape[1]), F32)
    sums = jnp.concatenate(sums + [filler], axis=0).astype(BF16)
    for ref in (mine_ref, peer_ref):
        ref[count * capacity :, : sums.shape[1]] = sums


def silu(value):
    return value / (1.0 + jnp.exp(-value))


def expert_kernel(mine_ref, peer_ref, up_hbm, down_hbm, mine_out, peer_out, up, down, active, up_sem, down_sem):
    half = mine_out.shape[0]
    width = mine_out.shape[1]
    units = down_hbm.shape[0]
    tiles = units // 128
    parts = down.shape[0]
    wide = width // parts
    copies = []
    for t in range(tiles):
        pair = []
        for s in range(2):
            at = pl.ds(s * units + t * 128, 128)
            pair.append(pltpu.make_async_copy(up_hbm.at[:, at], up.at[2 * t + s], up_sem.at[2 * t + s]))
        copies.append(pair)
    downs = [
        pltpu.make_async_copy(down_hbm.at[:, pl.ds(p * wide, wide)], down.at[p], down_sem.at[p])
        for p in range(parts)
    ]
    for pair in copies:
        for c in pair:
            c.start()
    for c in downs:
        c.start()
    rows = jnp.concatenate([mine_ref[:half, :], peer_ref[:half, :]], axis=0)
    for t in range(tiles):
        for c in copies[t]:
            c.wait()
        weight = jnp.concatenate([up[2 * t], up[2 * t + 1]], axis=1)
        inner = jnp.dot(rows, weight, preferred_element_type=F32)
        active[:, t * 128 : (t + 1) * 128] = (silu(inner[:, :128]) * inner[:, 128:]).astype(BF16)
    for p in range(parts):
        downs[p].wait()
        result = jnp.dot(active[...], down[p], preferred_element_type=F32).astype(BF16)
        mine_out[:, p * wide : (p + 1) * wide] = result[:half]
        peer_out[:, p * wide : (p + 1) * wide] = result[half:]


def shared_kernel(count, width, *refs):
    blocks, (weights_hbm, out_ref, weights, sems) = refs[:count], refs[count:]
    copies = [pltpu.make_async_copy(weights_hbm.at[i], weights.at[i], sems.at[i]) for i in range(3)]
    for c in copies:
        c.start()
    states = jnp.concatenate([b[:, :width] for b in blocks], axis=0)
    across = (((1,), (1,)), ((), ()))
    copies[0].wait()
    gate = lax.dot_general(states, weights[0], across, preferred_element_type=F32)
    copies[1].wait()
    up = lax.dot_general(states, weights[1], across, preferred_element_type=F32)
    active = (silu(gate) * up).astype(BF16)
    copies[2].wait()
    out_ref[...] = jnp.dot(active, weights[2], preferred_element_type=F32)


def mix_kernel(count, width, experts, capacity, *refs):
    blocks, (mine_ref, peer_ref, shared_ref), outs = refs[:count], refs[count : count + 3], refs[count + 3 :]
    me, peer = my_seat()
    rows = blocks[0].shape[0]
    for i, block in enumerate(blocks):
        match, slot = matches(block, width, experts, capacity)
        mine, theirs = columns_of(block, width, [me, peer])
        mixing = jnp.where(match, jnp.where(slot < capacity, mine, theirs), 0.0).astype(BF16)
        at = slice(i * capacity, (i + 1) * capacity)
        results = jnp.concatenate([mine_ref[at, :], peer_ref[at, :]], axis=0)
        total = shared_ref[i * rows : (i + 1) * rows, :] + jnp.dot(
            mixing, results, preferred_element_type=F32
        )
        outs[i][...] = total.astype(outs[i].dtype)


def penalty_kernel(experts, scale, *refs):
    sums, out_ref = refs[:-1], refs[-1]
    own = jnp.concatenate([s[...] for s in sums[0::2]], axis=0)
    peer = jnp.concatenate([s[...] for s in sums[1::2]], axis=0)
    seats = own.shape[0]
    seat = lax.axis_index("expert")
    order = (iota((seats, seats), 0) == (iota((seats, seats), 1) ^ seat)).astype(F32).astype(BF16)
    own = jnp.dot(order, own, preferred_element_type=F32)
    peer = jnp.dot(order, peer, preferred_element_type=F32)

    def part(array, i):
        return array[:, i * experts : (i + 1) * experts]

    load = jnp.sum(part(own, 2) + part(peer, 2), axis=0, keepdims=True)
    mass = (part(own, 3) + part(own, 4) + part(own, 5)) + (part(peer, 3) + part(peer, 4) + part(peer, 5))
    mass = jnp.sum(mass, axis=0, keepdims=True)
    out_ref[...] = jnp.sum(load * mass, axis=1, keepdims=True) * experts / scale


def call(kernel, out_shape, where, flops, nbytes, mib, scratch=()):
    spaces = {"v": pltpu.VMEM, "s": pltpu.SMEM, "h": pltpu.HBM}
    many = isinstance(out_shape, (list, tuple))
    specs = {"v": VMEM, "s": SMEM, "h": pl.BlockSpec(memory_space=pltpu.HBM)}

    def vmem(x):
        return pltpu.VMEM(x.shape, x.dtype)

    run = pl.pallas_call(
        kernel,
        out_shape=[vmem(x) for x in out_shape] if many else vmem(out_shape),
        in_specs=[specs[w] for w in where],
        out_specs=[VMEM] * len(out_shape) if many else VMEM,
        scratch_shapes=list(scratch),
        cost_estimate=pl.CostEstimate(flops=flops, bytes_accessed=nbytes, transcendentals=0),
        compiler_params=pltpu.CompilerParams(vmem_limit_bytes=mib << 20),
    )

    def go(*args):
        args = [
            a if w == "s" else pltpu.with_memory_space_constraint(a, spaces[w])
            for a, w in zip(args, where)
        ]
        return run(*args)

    return go


def chunks_of(steps):
    half = max(steps // 2, 1)
    return [range(0, half), range(half, steps)]


def on_device(
    hidden_state,
    norm_gain,
    router_weight,
    expert_ids,
    live_counts,
    routed_gate_up,
    routed_down,
    shared_weights,
):
    tok_rows, width = hidden_state.shape
    choose = expert_ids.shape[1]
    hidden_units = routed_down.shape[1]
    expert_count = lax.axis_size("expert")
    sub_count = lax.axis_size("sub")
    devices = expert_count * sub_count
    all_experts = routed_gate_up.shape[0] * devices
    assert routed_gate_up.shape[0] == 1 and sub_count == 2
    all_tokens = tok_rows * devices
    capacity = (tok_rows * choose * 4 + 3 * all_experts - 1) // (3 * all_experts)
    shape = jax.ShapeDtypeStruct

    def cross(block, step):
        return lax.ppermute(block, "expert", [(e, e ^ step) for e in range(expert_count)])

    def swap(block):
        return lax.ppermute(block, "sub", [(0, 1), (1, 0)])

    lanes = -(-6 * all_experts // 128) * 128
    packet = call(
        route_kernel,
        shape((tok_rows, width + lanes), BF16),
        "svvvv",
        2 * tok_rows * width * all_experts,
        4 * tok_rows * width,
        8,
    )(live_counts, hidden_state, norm_gain.reshape(1, width), router_weight.T, expert_ids.T)

    steps = expert_count // 2
    chunks = chunks_of(steps)
    direct = [packet] + [cross(packet, 2 * j) for j in range(1, steps)]
    near = [cross(direct[j], 1) for j in range(steps)]

    gate_up, down = routed_gate_up[0], routed_down[0]
    shared_rows = jnp.swapaxes(shared_weights, 1, 2)
    keeps, leaves, sums = [None] * steps, [None] * steps, []
    for chunk in chunks:
        blocks = [b for j in chunk for b in (direct[j], near[j])]
        count = len(blocks)
        picked = shape((count * capacity + 16, width), BF16)
        results = shape((count * capacity, width), BF16)
        mine, theirs = call(
            functools.partial(pick_kernel, count, width, all_experts, capacity),
            (picked, picked),
            "v" * count,
            4 * count * tok_rows * capacity * width,
            8 * count * capacity * width,
            12,
        )(*blocks)
        theirs = swap(theirs)
        shared = call(
            functools.partial(shared_kernel, count, width),
            shape((count * tok_rows, width), F32),
            "v" * count + "h",
            6 * count * tok_rows * width * shared_rows.shape[1],
            6 * width * shared_rows.shape[1],
            24,
            [pltpu.VMEM(shared_rows.shape, BF16), pltpu.SemaphoreType.DMA((3,))],
        )(*blocks, shared_rows)
        sums += [x[count * capacity :][:count, :lanes] for x in (mine, theirs)]
        parts = 4
        mine, theirs = call(
            expert_kernel,
            (results, results),
            "vvhh",
            12 * count * capacity * width * hidden_units,
            6 * width * hidden_units,
            32,
            [
                pltpu.VMEM((2 * hidden_units // 128, width, 128), BF16),
                pltpu.VMEM((parts, hidden_units, width // parts), BF16),
                pltpu.VMEM((2 * count * capacity, hidden_units), BF16),
                pltpu.SemaphoreType.DMA((2 * hidden_units // 128,)),
                pltpu.SemaphoreType.DMA((parts,)),
            ],
        )(mine, theirs, gate_up, down)
        theirs = swap(theirs)
        tokens = (tok_rows, width)
        totals = call(
            functools.partial(mix_kernel, count, width, all_experts, capacity),
            [shape(tokens, F32), shape(tokens, BF16)] * (count // 2),
            "v" * (count + 3),
            4 * count * tok_rows * capacity * width,
            8 * count * tok_rows * width,
            16,
        )(*blocks, mine, theirs, shared)
        for i, j in enumerate(chunk):
            keeps[j], leaves[j] = totals[2 * i], totals[2 * i + 1]

    mixed = None
    for j in reversed(range(steps)):
        both = keeps[j] + cross(leaves[j], 1).astype(F32)
        term = both if j == 0 else cross(both.astype(BF16), 2 * j).astype(F32)
        mixed = term if mixed is None else mixed + term
    mixed = mixed.astype(BF16)

    penalty = call(
        functools.partial(penalty_kernel, all_experts, choose * float(all_tokens) * float(all_tokens)),
        shape((1, 1), F32),
        "v" * len(sums),
        0,
        0,
        4,
    )(*sums)
    return (mixed, penalty.reshape(1))


def solution(mesh):
    placed = (
        P(("groups", "expert", "sub"), None),
        P(),
        P(),
        P(("groups", "expert", "sub"), None),
        P(("groups", "expert", "sub")),
        P(("expert", "sub"), None, None),
        P(("expert", "sub"), None, None),
        P(None, None, "expert"),
    )

    return jax.shard_map(
        on_device,
        mesh=mesh,
        in_specs=placed,
        out_specs=(P(("groups", "expert", "sub"), None), P("groups")),
        check_vma=False,
    )
```

profile of v0, /device:TPU:0, one launch (start us, length us, event | category | flops | bytes accessed | tf_op | source)
XLA Modules:
  0.0 122.2 jit_solution(14078725565681120561)
XLA Ops:
  1.3 0.9 copy-done
  5.1 5.1 %collective-permute-start.2 = (bf16[64,2176]{1,0:T(8,128)(2,1)S(1)}, bf16[64,2176]{1,0:T(8,128)(2,1)S(1)}, u32[]{:S(2)}, u32[]{:S(2)}) collective-permute-start(bf16[64,2176]{1,0:T(8,128)(2,1)S(1)} %shard_map.95.refs_0_), channel_id=1, source_target_pairs={{0,12},{2,14},{4,8},{6,10},{8,4},{10,6},{12,0},{14,2},{1,13},{3,15... | collective-permute-start | bytes 835592 | tf_op jit(solution)/shard_map/ppermute | solution.py:256
  10.2 7.6 %collective-permute-done.2.refs_2_ = bf16[64,2176]{1,0:T(8,128)(2,1)S(1)} collective-permute-done((bf16[64,2176]{1,0:T(8,128)(2,1)S(1)}, bf16[64,2176]{1,0:T(8,128)(2,1)S(1)}, u32[]{:S(2)}, u32[]{:S(2)}) %collective-permute-start.2) | collective-permute-done | bytes 278560 | tf_op jit(solution)/shard_map/ppermute | solution.py:256
  17.8 1.7 %collective-permute-start.3 = (bf16[64,2176]{1,0:T(8,128)(2,1)S(1)}, bf16[64,2176]{1,0:T(8,128)(2,1)S(1)}, u32[]{:S(2)}, u32[]{:S(2)}) collective-permute-start(bf16[64,2176]{1,0:T(8,128)(2,1)S(1)} %collective-permute-done.2.refs_2_), channel_id=1, source_target_pairs={{0,2},{2,0},{4,6},{6,4},{8,10},{10,8},{12,14},{14,12},{1,3},{3,1},... | collective-permute-start | bytes 835592 | tf_op jit(solution)/shard_map/ppermute | solution.py:256
  19.5 14.4 %collective-permute-done.refs_0_ = bf16[64,2176]{1,0:T(8,128)(2,1)S(1)} collective-permute-done((bf16[64,2176]{1,0:T(8,128)(2,1)S(1)}, bf16[64,2176]{1,0:T(8,128)(2,1)S(1)}, u32[]{:S(2)}, u32[]{:S(2)}) %collective-permute-start) | collective-permute-done | bytes 278560 | tf_op jit(solution)/shard_map/ppermute | solution.py:256
  33.9 1.5 %collective-permute-start.1 = (bf16[64,2176]{1,0:T(8,128)(2,1)S(1)}, bf16[64,2176]{1,0:T(8,128)(2,1)S(1)}, u32[]{:S(2)}, u32[]{:S(2)}) collective-permute-start(bf16[64,2176]{1,0:T(8,128)(2,1)S(1)} %collective-permute-done.refs_0_), channel_id=1, source_target_pairs={{0,2},{2,0},{4,6},{6,4},{8,10},{10,8},{12,14},{14,12},{1,3},{3,1},... | collective-permute-start | bytes 835592 | tf_op jit(solution)/shard_map/ppermute | solution.py:256
  35.4 6.2 %collective-permute-done.1.refs_1_ = bf16[64,2176]{1,0:T(8,128)(2,1)S(1)} collective-permute-done((bf16[64,2176]{1,0:T(8,128)(2,1)S(1)}, bf16[64,2176]{1,0:T(8,128)(2,1)S(1)}, u32[]{:S(2)}, u32[]{:S(2)}) %collective-permute-start.1) | collective-permute-done | bytes 278560 | tf_op jit(solution)/shard_map/ppermute | solution.py:256
  42.4 1.6 %collective-permute-start.10 = (bf16[64,2176]{1,0:T(8,128)(2,1)S(1)}, bf16[64,2176]{1,0:T(8,128)(2,1)S(1)}, u32[]{:S(2)}, u32[]{:S(2)}) collective-permute-start(bf16[64,2176]{1,0:T(8,128)(2,1)S(1)} %shard_map.95.refs_0_), channel_id=1, source_target_pairs={{0,2},{2,0},{4,6},{6,4},{8,10},{10,8},{12,14},{14,12},{1,3},{3,1},... | collective-permute-start | bytes 835592 | tf_op jit(solution)/shard_map/ppermute | solution.py:256
  44.5 7.5 %collective-permute-done.10.refs_1_ = bf16[64,2176]{1,0:T(8,128)(2,1)S(1)} collective-permute-done((bf16[64,2176]{1,0:T(8,128)(2,1)S(1)}, bf16[64,2176]{1,0:T(8,128)(2,1)S(1)}, u32[]{:S(2)}, u32[]{:S(2)}) %collective-permute-start.10) | collective-permute-done | bytes 278560 | tf_op jit(solution)/shard_map/ppermute | solution.py:256
  52.0 5.4 %collective-permute-done.12.refs_3_ = bf16[64,2176]{1,0:T(8,128)(2,1)S(1)} collective-permute-done((bf16[64,2176]{1,0:T(8,128)(2,1)S(1)}, bf16[64,2176]{1,0:T(8,128)(2,1)S(1)}, u32[]{:S(2)}, u32[]{:S(2)}) %collective-permute-start.12) | collective-permute-done | bytes 278560 | tf_op jit(solution)/shard_map/ppermute | solution.py:256
  58.2 11.8 %shard_map.97 = (bf16[128,2048]{1,0:T(8,128)(2,1)S(1)}, bf16[128,2048]{1,0:T(8,128)(2,1)S(1)}) custom-call(bf16[144,2048]{1,0:T(8,128)(2,1)S(1)} %get-tuple-element.18.mine_ref, bf16[144,2048]{1,0:T(8,128)(2,1)S(1)} %collective-permute-done.4.peer_ref, bf16[2048,2816]{1,0:T(8,128)(2,1)} %bitcast.11, bf16[1408,2048]{1,0:T(8,128)(2,1)} %bitcast.13), custom_call_target="tpu_custom_call" | custom-call | flops 4429185024 | bytes 17301504 | tf_op jit(solution)/shard_map/pallas_call | solution.py:223
  70.5 11.9 %shard_map.101 = (bf16[128,2048]{1,0:T(8,128)(2,1)S(1)}, bf16[128,2048]{1,0:T(8,128)(2,1)S(1)}) custom-call(bf16[144,2048]{1,0:T(8,128)(2,1)S(1)} %get-tuple-element.26.mine_ref, bf16[144,2048]{1,0:T(8,128)(2,1)S(1)} %collective-permute-done.13.peer_ref, bf16[2048,2816]{1,0:T(8,128)(2,1)} %bitcast.12, bf16[1408,2048]{1,0:T(8,128)(2,1)} %bitcast.14), custom_call_target="tpu_custom_call" | custom-call | flops 4429185024 | bytes 17301504 | tf_op jit(solution)/shard_map/pallas_call | solution.py:223
  82.6 3.6 %shard_map.98.refs_6_ = f32[256,2048]{1,0:T(8,128)S(1)} custom-call(bf16[64,2176]{1,0:T(8,128)(2,1)S(1)} %collective-permute-done.refs_0_, bf16[64,2176]{1,0:T(8,128)(2,1)S(1)} %collective-permute-done.1.refs_1_, bf16[64,2176]{1,0:T(8,128)(2,1)S(1)} %collective-permute-done.2.refs_2_, bf16[64,2176]{1,0:T(8,128)(2,1)S(1)} %collective-permute-done.3.refs_3_, ...), custom_call_target="tpu_custom_call" | custom-call | flops 1107296256 | bytes 4325376 | tf_op jit(solution)/shard_map/pallas_call | solution.py:223
  86.7 1.6 %collective-permute-start.6 = (bf16[64,2048]{1,0:T(8,128)(2,1)S(1)}, bf16[64,2048]{1,0:T(8,128)(2,1)S(1)}, u32[]{:S(2)}, u32[]{:S(2)}) collective-permute-start(bf16[64,2048]{1,0:T(8,128)(2,1)S(1)} %get-tuple-element.23), channel_id=1, source_target_pairs={{0,2},{2,0},{4,6},{6,4},{8,10},{10,8},{12,14},{14,12},{1,3},{3,1},... | collective-permute-start | bytes 786440 | tf_op jit(solution)/shard_map/ppermute | solution.py:256
  88.3 3.6 %shard_map.102.refs_6_ = f32[256,2048]{1,0:T(8,128)S(1)} custom-call(bf16[64,2176]{1,0:T(8,128)(2,1)S(1)} %shard_map.95.refs_0_, bf16[64,2176]{1,0:T(8,128)(2,1)S(1)} %collective-permute-done.10.refs_1_, bf16[64,2176]{1,0:T(8,128)(2,1)S(1)} %collective-permute-done.11.refs_2_, bf16[64,2176]{1,0:T(8,128)(2,1)S(1)} %collective-permute-done.12.refs_3_, ...), custom_call_target="tpu_custom_call" | custom-call | flops 1107296256 | bytes 4325376 | tf_op jit(solution)/shard_map/pallas_call | solution.py:223
  93.0 1.6 %collective-permute-start.15 = (bf16[64,2048]{1,0:T(8,128)(2,1)S(1)}, bf16[64,2048]{1,0:T(8,128)(2,1)S(1)}, u32[]{:S(2)}, u32[]{:S(2)}) collective-permute-start(bf16[64,2048]{1,0:T(8,128)(2,1)S(1)} %get-tuple-element.31), channel_id=1, source_target_pairs={{0,2},{2,0},{4,6},{6,4},{8,10},{10,8},{12,14},{14,12},{1,3},{3,1},... | collective-permute-start | bytes 786440 | tf_op jit(solution)/shard_map/ppermute | solution.py:256
  95.1 0.9 collective-permute-done.6
  96.0 2.3 %collective-permute-start.7 = (bf16[64,2048]{1,0:T(8,128)(2,1)S(1)}, bf16[64,2048]{1,0:T(8,128)(2,1)S(1)}, u32[]{:S(2)}, u32[]{:S(2)}) collective-permute-start(bf16[64,2048]{1,0:T(8,128)(2,1)S(1)} %add_convert_fusion.3), channel_id=1, source_target_pairs={{0,12},{2,14},{4,8},{6,10},{8,4},{10,6},{12,0},{14,2},{1,13},{3,15... | collective-permute-start | bytes 786440 | tf_op jit(solution)/shard_map/ppermute | solution.py:256
  98.3 3.2 %collective-permute-done.8 = bf16[64,2048]{1,0:T(8,128)(2,1)S(1)} collective-permute-done((bf16[64,2048]{1,0:T(8,128)(2,1)S(1)}, bf16[64,2048]{1,0:T(8,128)(2,1)S(1)}, u32[]{:S(2)}, u32[]{:S(2)}) %collective-permute-start.8) | collective-permute-done | bytes 262176 | tf_op jit(solution)/shard_map/ppermute | solution.py:256
  101.6 1.6 %collective-permute-start.9 = (bf16[64,2048]{1,0:T(8,128)(2,1)S(1)}, bf16[64,2048]{1,0:T(8,128)(2,1)S(1)}, u32[]{:S(2)}, u32[]{:S(2)}) collective-permute-start(bf16[64,2048]{1,0:T(8,128)(2,1)S(1)} %add_convert_fusion.2), channel_id=1, source_target_pairs={{0,8},{2,10},{4,12},{6,14},{8,0},{10,2},{12,4},{14,6},{1,9},{3,11}... | collective-permute-start | bytes 786440 | tf_op jit(solution)/shard_map/ppermute | solution.py:256
  103.2 4.0 %collective-permute-done.15 = bf16[64,2048]{1,0:T(8,128)(2,1)S(1)} collective-permute-done((bf16[64,2048]{1,0:T(8,128)(2,1)S(1)}, bf16[64,2048]{1,0:T(8,128)(2,1)S(1)}, u32[]{:S(2)}, u32[]{:S(2)}) %collective-permute-start.15) | collective-permute-done | bytes 262176 | tf_op jit(solution)/shard_map/ppermute | solution.py:256
  108.3 4.0 %collective-permute-done.17 = bf16[64,2048]{1,0:T(8,128)(2,1)S(1)} collective-permute-done((bf16[64,2048]{1,0:T(8,128)(2,1)S(1)}, bf16[64,2048]{1,0:T(8,128)(2,1)S(1)}, u32[]{:S(2)}, u32[]{:S(2)}) %collective-permute-start.17) | collective-permute-done | bytes 262176 | tf_op jit(solution)/shard_map/ppermute | solution.py:256
  112.3 7.9 %collective-permute-done.9 = bf16[64,2048]{1,0:T(8,128)(2,1)S(1)} collective-permute-done((bf16[64,2048]{1,0:T(8,128)(2,1)S(1)}, bf16[64,2048]{1,0:T(8,128)(2,1)S(1)}, u32[]{:S(2)}, u32[]{:S(2)}) %collective-permute-start.9) | collective-permute-done | bytes 262176 | tf_op jit(solution)/shard_map/ppermute | solution.py:256
  120.3 0.9 add_convert_fusion
  (38 shorter events, 8.8 us)
Async XLA Ops:
  1.3 1.0 copy-start
  2.2 0.8 copy-start.1
  3.1 0.7 copy-start.2
  3.8 0.7 copy-start.3
  5.1 12.7 %collective-permute-start.2 = (bf16[64,2176]{1,0:T(8,128)(2,1)S(1)}, bf16[64,2176]{1,0:T(8,128)(2,1)S(1)}, u32[]{:S(2)}, u32[]{:S(2)}) collective-permute-start(bf16[64,2176]{1,0:T(8,128)(2,1)S(1)} %shard_map.95.refs_0_), channel_id=1, source_target_pairs={{0,12},{2,14},{4,8},{6,10},{8,4},{10,6},{12,0},{14,2},{1,13},{3,15... | collective-permute-start | bytes 835592 | tf_op jit(solution)/shard_map/ppermute | solution.py:256
  10.2 23.7 %collective-permute-start = (bf16[64,2176]{1,0:T(8,128)(2,1)S(1)}, bf16[64,2176]{1,0:T(8,128)(2,1)S(1)}, u32[]{:S(2)}, u32[]{:S(2)}) collective-permute-start(bf16[64,2176]{1,0:T(8,128)(2,1)S(1)} %shard_map.95.refs_0_), channel_id=1, source_target_pairs={{0,8},{2,10},{4,12},{6,14},{8,0},{10,2},{12,4},{14,6},{1,9},{3,11}... | collective-permute-start | bytes 835592 | tf_op jit(solution)/shard_map/ppermute | solution.py:256
  17.8 17.6 %collective-permute-start.3 = (bf16[64,2176]{1,0:T(8,128)(2,1)S(1)}, bf16[64,2176]{1,0:T(8,128)(2,1)S(1)}, u32[]{:S(2)}, u32[]{:S(2)}) collective-permute-start(bf16[64,2176]{1,0:T(8,128)(2,1)S(1)} %collective-permute-done.2.refs_2_), channel_id=1, source_target_pairs={{0,2},{2,0},{4,6},{6,4},{8,10},{10,8},{12,14},{14,12},{1,3},{3,1},... | collective-permute-start | bytes 835592 | tf_op jit(solution)/shard_map/ppermute | solution.py:256
  33.9 7.7 %collective-permute-start.1 = (bf16[64,2176]{1,0:T(8,128)(2,1)S(1)}, bf16[64,2176]{1,0:T(8,128)(2,1)S(1)}, u32[]{:S(2)}, u32[]{:S(2)}) collective-permute-start(bf16[64,2176]{1,0:T(8,128)(2,1)S(1)} %collective-permute-done.refs_0_), channel_id=1, source_target_pairs={{0,2},{2,0},{4,6},{6,4},{8,10},{10,8},{12,14},{14,12},{1,3},{3,1},... | collective-permute-start | bytes 835592 | tf_op jit(solution)/shard_map/ppermute | solution.py:256
  35.4 8.6 %collective-permute-start.11 = (bf16[64,2176]{1,0:T(8,128)(2,1)S(1)}, bf16[64,2176]{1,0:T(8,128)(2,1)S(1)}, u32[]{:S(2)}, u32[]{:S(2)}) collective-permute-start(bf16[64,2176]{1,0:T(8,128)(2,1)S(1)} %shard_map.95.refs_0_), channel_id=1, source_target_pairs={{0,4},{2,6},{4,0},{6,2},{8,12},{10,14},{12,8},{14,10},{1,5},{3,7},... | collective-permute-start | bytes 835592 | tf_op jit(solution)/shard_map/ppermute | solution.py:256
  42.3 15.9 %collective-permute-start.4 = (bf16[144,2048]{1,0:T(8,128)(2,1)S(1)}, bf16[144,2048]{1,0:T(8,128)(2,1)S(1)}, u32[]{:S(2)}, u32[]{:S(2)}) collective-permute-start(bf16[144,2048]{1,0:T(8,128)(2,1)S(1)} %get-tuple-element.19), channel_id=1, source_target_pairs={{0,1},{1,0},{2,3},{3,2},{4,5},{5,4},{6,7},{7,6},{8,9},{9,8},{10,11... | collective-permute-start | bytes 1769480 | tf_op jit(solution)/shard_map/ppermute | solution.py:259
  42.4 9.6 %collective-permute-start.10 = (bf16[64,2176]{1,0:T(8,128)(2,1)S(1)}, bf16[64,2176]{1,0:T(8,128)(2,1)S(1)}, u32[]{:S(2)}, u32[]{:S(2)}) collective-permute-start(bf16[64,2176]{1,0:T(8,128)(2,1)S(1)} %shard_map.95.refs_0_), channel_id=1, source_target_pairs={{0,2},{2,0},{4,6},{6,4},{8,10},{10,8},{12,14},{14,12},{1,3},{3,1},... | collective-permute-start | bytes 835592 | tf_op jit(solution)/shard_map/ppermute | solution.py:256
  44.0 13.4 %collective-permute-start.12 = (bf16[64,2176]{1,0:T(8,128)(2,1)S(1)}, bf16[64,2176]{1,0:T(8,128)(2,1)S(1)}, u32[]{:S(2)}, u32[]{:S(2)}) collective-permute-start(bf16[64,2176]{1,0:T(8,128)(2,1)S(1)} %collective-permute-done.11.refs_2_), channel_id=1, source_target_pairs={{0,2},{2,0},{4,6},{6,4},{8,10},{10,8},{12,14},{14,12},{1,3},{3,1},... | collective-permute-start | bytes 835592 | tf_op jit(solution)/shard_map/ppermute | solution.py:256
  58.1 12.4 %collective-permute-start.13 = (bf16[144,2048]{1,0:T(8,128)(2,1)S(1)}, bf16[144,2048]{1,0:T(8,128)(2,1)S(1)}, u32[]{:S(2)}, u32[]{:S(2)}) collective-permute-start(bf16[144,2048]{1,0:T(8,128)(2,1)S(1)} %get-tuple-element.27), channel_id=1, source_target_pairs={{0,1},{1,0},{2,3},{3,2},{4,5},{5,4},{6,7},{7,6},{8,9},{9,8},{10,11... | collective-permute-start | bytes 1769480 | tf_op jit(solution)/shard_map/ppermute | solution.py:259
  70.0 16.2 %collective-permute-start.5 = (bf16[128,2048]{1,0:T(8,128)(2,1)S(1)}, bf16[128,2048]{1,0:T(8,128)(2,1)S(1)}, u32[]{:S(2)}, u32[]{:S(2)}) collective-permute-start(bf16[128,2048]{1,0:T(8,128)(2,1)S(1)} %get-tuple-element.21), channel_id=1, source_target_pairs={{0,1},{1,0},{2,3},{3,2},{4,5},{5,4},{6,7},{7,6},{8,9},{9,8},{10,11... | collective-permute-start | bytes 1572872 | tf_op jit(solution)/shard_map/ppermute | solution.py:259
  82.5 10.0 %collective-permute-start.14 = (bf16[128,2048]{1,0:T(8,128)(2,1)S(1)}, bf16[128,2048]{1,0:T(8,128)(2,1)S(1)}, u32[]{:S(2)}, u32[]{:S(2)}) collective-permute-start(bf16[128,2048]{1,0:T(8,128)(2,1)S(1)} %get-tuple-element.29), channel_id=1, source_target_pairs={{0,1},{1,0},{2,3},{3,2},{4,5},{5,4},{6,7},{7,6},{8,9},{9,8},{10,11... | collective-permute-start | bytes 1572872 | tf_op jit(solution)/shard_map/ppermute | solution.py:259
  86.7 9.2 %collective-permute-start.6 = (bf16[64,2048]{1,0:T(8,128)(2,1)S(1)}, bf16[64,2048]{1,0:T(8,128)(2,1)S(1)}, u32[]{:S(2)}, u32[]{:S(2)}) collective-permute-start(bf16[64,2048]{1,0:T(8,128)(2,1)S(1)} %get-tuple-element.23), channel_id=1, source_target_pairs={{0,2},{2,0},{4,6},{6,4},{8,10},{10,8},{12,14},{14,12},{1,3},{3,1},... | collective-permute-start | bytes 786440 | tf_op jit(solution)/shard_map/ppermute | solution.py:256
  91.9 9.7 %collective-permute-start.8 = (bf16[64,2048]{1,0:T(8,128)(2,1)S(1)}, bf16[64,2048]{1,0:T(8,128)(2,1)S(1)}, u32[]{:S(2)}, u32[]{:S(2)}) collective-permute-start(bf16[64,2048]{1,0:T(8,128)(2,1)S(1)} %get-tuple-element.25), channel_id=1, source_target_pairs={{0,2},{2,0},{4,6},{6,4},{8,10},{10,8},{12,14},{14,12},{1,3},{3,1},... | collective-permute-start | bytes 786440 | tf_op jit(solution)/shard_map/ppermute | solution.py:256
  93.0 14.2 %collective-permute-start.15 = (bf16[64,2048]{1,0:T(8,128)(2,1)S(1)}, bf16[64,2048]{1,0:T(8,128)(2,1)S(1)}, u32[]{:S(2)}, u32[]{:S(2)}) collective-permute-start(bf16[64,2048]{1,0:T(8,128)(2,1)S(1)} %get-tuple-element.31), channel_id=1, source_target_pairs={{0,2},{2,0},{4,6},{6,4},{8,10},{10,8},{12,14},{14,12},{1,3},{3,1},... | collective-permute-start | bytes 786440 | tf_op jit(solution)/shard_map/ppermute | solution.py:256
  94.5 17.8 %collective-permute-start.17 = (bf16[64,2048]{1,0:T(8,128)(2,1)S(1)}, bf16[64,2048]{1,0:T(8,128)(2,1)S(1)}, u32[]{:S(2)}, u32[]{:S(2)}) collective-permute-start(bf16[64,2048]{1,0:T(8,128)(2,1)S(1)} %get-tuple-element.33), channel_id=1, source_target_pairs={{0,2},{2,0},{4,6},{6,4},{8,10},{10,8},{12,14},{14,12},{1,3},{3,1},... | collective-permute-start | bytes 786440 | tf_op jit(solution)/shard_map/ppermute | solution.py:256
  96.0 16.3 %collective-permute-start.7 = (bf16[64,2048]{1,0:T(8,128)(2,1)S(1)}, bf16[64,2048]{1,0:T(8,128)(2,1)S(1)}, u32[]{:S(2)}, u32[]{:S(2)}) collective-permute-start(bf16[64,2048]{1,0:T(8,128)(2,1)S(1)} %add_convert_fusion.3), channel_id=1, source_target_pairs={{0,12},{2,14},{4,8},{6,10},{8,4},{10,6},{12,0},{14,2},{1,13},{3,15... | collective-permute-start | bytes 786440 | tf_op jit(solution)/shard_map/ppermute | solution.py:256
  101.6 18.6 %collective-permute-start.9 = (bf16[64,2048]{1,0:T(8,128)(2,1)S(1)}, bf16[64,2048]{1,0:T(8,128)(2,1)S(1)}, u32[]{:S(2)}, u32[]{:S(2)}) collective-permute-start(bf16[64,2048]{1,0:T(8,128)(2,1)S(1)} %add_convert_fusion.2), channel_id=1, source_target_pairs={{0,8},{2,10},{4,12},{6,14},{8,0},{10,2},{12,4},{14,6},{1,9},{3,11}... | collective-permute-start | bytes 786440 | tf_op jit(solution)/shard_map/ppermute | solution.py:256
  107.2 13.0 %collective-permute-start.16 = (bf16[64,2048]{1,0:T(8,128)(2,1)S(1)}, bf16[64,2048]{1,0:T(8,128)(2,1)S(1)}, u32[]{:S(2)}, u32[]{:S(2)}) collective-permute-start(bf16[64,2048]{1,0:T(8,128)(2,1)S(1)} %add_convert_fusion.1), channel_id=1, source_target_pairs={{0,4},{2,6},{4,0},{6,2},{8,12},{10,14},{12,8},{14,10},{1,5},{3,7},... | collective-permute-start | bytes 786440 | tf_op jit(solution)/shard_map/ppermute | solution.py:256
where the time goes:
time: 123 us; the launch traced here: 122 us
  waiting for transfers between devices  61.2 us (50%)
  Pallas kernels  34.3 us (28%)
  starting transfers between devices  20 us (16%)
  local copies, waits for them, and re-layouts  3.17 us (3%)
  between operations  2.58 us (2%)
    ppermute x14, waiting for transfers between devices, cross(): lax.ppermute(block, 'expert', [(e, e ^ step) for e in range(expert_count)])  61.2 us
    pallas_call x10, Pallas kernels, go(): return run(*args)  34.3 us
    ppermute x14, starting transfers between devices, cross(): lax.ppermute(block, 'expert', [(e, e ^ step) for e in range(expert_count)])  19.2 us
    unnamed x8, local copies, waits for them, and re-layouts  3.16 us
  transfers between devices with their start and end apart: 18, of which 10 were waited for; matrix products, arithmetic and copies ran while one was open for 0% of the time, Pallas kernels for 28%

commit v1 on v0

--- a/solution.py
+++ b/solution.py
@@ -32,7 +32,13 @@
     return me, me ^ 1
 
 
-def route_kernel(live_ref, hidden_ref, gain_ref, router_ref, ids_ref, packet_ref):
+def route_kernel(live_ref, hidden_hbm, gain_hbm, router_hbm, ids_hbm, packet_ref, hidden_ref, gain_ref, router_ref, ids_ref, sems):
+    pairs = ((hidden_hbm, hidden_ref), (gain_hbm, gain_ref), (router_hbm, router_ref), (ids_hbm, ids_ref))
+    copies = [pltpu.make_async_copy(x, y, sems.at[i]) for i, (x, y) in enumerate(pairs)]
+    for c in copies:
+        c.start()
+    for c in copies:
+        c.wait()
     rows, width = hidden_ref.shape
     experts = router_ref.shape[0]
     lanes = packet_ref.shape[1] - width
@@ -109,57 +115,40 @@
     return value / (1.0 + jnp.exp(-value))
 
 
-def expert_kernel(mine_ref, peer_ref, up_hbm, down_hbm, mine_out, peer_out, up, down, active, up_sem, down_sem):
-    half = mine_out.shape[0]
-    width = mine_out.shape[1]
-    units = down_hbm.shape[0]
-    tiles = units // 128
-    parts = down.shape[0]
-    wide = width // parts
-    copies = []
-    for t in range(tiles):
-        pair = []
-        for s in range(2):
-            at = pl.ds(s * units + t * 128, 128)
-            pair.append(pltpu.make_async_copy(up_hbm.at[:, at], up.at[2 * t + s], up_sem.at[2 * t + s]))
-        copies.append(pair)
-    downs = [
-        pltpu.make_async_copy(down_hbm.at[:, pl.ds(p * wide, wide)], down.at[p], down_sem.at[p])
-        for p in range(parts)
-    ]
-    for pair in copies:
-        for c in pair:
-            c.start()
-    for c in downs:
-        c.start()
-    rows = jnp.concatenate([mine_ref[:half, :], peer_ref[:half, :]], axis=0)
-    for t in range(tiles):
-        for c in copies[t]:
-            c.wait()
-        weight = jnp.concatenate([up[2 * t], up[2 * t + 1]], axis=1)
-        inner = jnp.dot(rows, weight, preferred_element_type=F32)
-        active[:, t * 128 : (t + 1) * 128] = (silu(inner[:, :128]) * inner[:, 128:]).astype(BF16)
-    for p in range(parts):
-        downs[p].wait()
-        result = jnp.dot(active[...], down[p], preferred_element_type=F32).astype(BF16)
-        mine_out[:, p * wide : (p + 1) * wide] = result[:half]
-        peer_out[:, p * wide : (p + 1) * wide] = result[half:]
-
-
-def shared_kernel(count, width, *refs):
-    blocks, (weights_hbm, out_ref, weights, sems) = refs[:count], refs[count:]
-    copies = [pltpu.make_async_copy(weights_hbm.at[i], weights.at[i], sems.at[i]) for i in range(3)]
+def load_kernel(*refs):
+    count = (len(refs) - 1) // 2
+    sems = refs[-1]
+    copies = [pltpu.make_async_copy(refs[i], refs[count + i], sems.at[i]) for i in range(count)]
     for c in copies:
         c.start()
+    for c in copies:
+        c.wait()
+
+
+def expert_kernel(mine_ref, peer_ref, up_ref, down_ref, mine_out, peer_out, active):
+    half, width = mine_out.shape
+    units = down_ref.shape[0]
+    rows = jnp.concatenate([mine_ref[:half, :], peer_ref[:half, :]], axis=0)
+    for at in range(0, units, 256):
+        to = min(at + 256, units)
+        gate = jnp.dot(rows, up_ref[:, at:to], preferred_element_type=F32)
+        up = jnp.dot(rows, up_ref[:, units + at : units + to], preferred_element_type=F32)
+        active[:, at:to] = (silu(gate) * up).astype(BF16)
+    for at in range(0, width, 512):
+        to = min(at + 512, width)
+        result = jnp.dot(active[...], down_ref[:, at:to], preferred_element_type=F32).astype(BF16)
+        mine_out[:, at:to] = result[:half]
+        peer_out[:, at:to] = result[half:]
+
+
+def shared_kernel(count, width, *refs):
+    blocks, (weights_ref, out_ref) = refs[:count], refs[count:]
     states = jnp.concatenate([b[:, :width] for b in blocks], axis=0)
     across = (((1,), (1,)), ((), ()))
-    copies[0].wait()
-    gate = lax.dot_general(states, weights[0], across, preferred_element_type=F32)
-    copies[1].wait()
-    up = lax.dot_general(states, weights[1], across, preferred_element_type=F32)
+    gate = lax.dot_general(states, weights_ref[0], across, preferred_element_type=F32)
+    up = lax.dot_general(states, weights_ref[1], across, preferred_element_type=F32)
     active = (silu(gate) * up).astype(BF16)
-    copies[2].wait()
-    out_ref[...] = jnp.dot(active, weights[2], preferred_element_type=F32)
+    out_ref[...] = jnp.dot(active, weights_ref[2], preferred_element_type=F32)
 
 
 def mix_kernel(count, width, experts, capacity, *refs):
@@ -178,13 +167,17 @@
         outs[i][...] = total.astype(outs[i].dtype)
 
 
-def penalty_kernel(experts, scale, *refs):
+def penalty_kernel(experts, scale, steps, *refs):
     sums, out_ref = refs[:-1], refs[-1]
     own = jnp.concatenate([s[...] for s in sums[0::2]], axis=0)
     peer = jnp.concatenate([s[...] for s in sums[1::2]], axis=0)
     seats = own.shape[0]
     seat = lax.axis_index("expert")
-    order = (iota((seats, seats), 0) == (iota((seats, seats), 1) ^ seat)).astype(F32).astype(BF16)
+    row = iota((seats, seats), 1)
+    step = jnp.zeros_like(row)
+    for r, k in enumerate(steps):
+        step = jnp.where(row == r, k, step)
+    order = (iota((seats, seats), 0) == (step ^ seat)).astype(F32).astype(BF16)
     own = jnp.dot(order, own, preferred_element_type=F32)
     peer = jnp.dot(order, peer, preferred_element_type=F32)
 
@@ -226,8 +219,7 @@
 
 
 def chunks_of(steps):
-    half = max(steps // 2, 1)
-    return [range(0, half), range(half, steps)]
+    return [list(range(0, steps, 2)), list(range(1, steps, 2))]
 
 
 def on_device(
@@ -262,10 +254,17 @@
     packet = call(
         route_kernel,
         shape((tok_rows, width + lanes), BF16),
-        "svvvv",
+        "shhhh",
         2 * tok_rows * width * all_experts,
         4 * tok_rows * width,
         8,
+        [
+            pltpu.VMEM((tok_rows, width), BF16),
+            pltpu.VMEM((1, width), F32),
+            pltpu.VMEM((all_experts, width), BF16),
+            pltpu.VMEM((choose, tok_rows), jnp.int32),
+            pltpu.SemaphoreType.DMA((4,)),
+        ],
     )(live_counts, hidden_state, norm_gain.reshape(1, width), router_weight.T, expert_ids.T)
 
     steps = expert_count // 2
@@ -273,8 +272,19 @@
     direct = [packet] + [cross(packet, 2 * j) for j in range(1, steps)]
     near = [cross(direct[j], 1) for j in range(steps)]
 
-    gate_up, down = routed_gate_up[0], routed_down[0]
-    shared_rows = jnp.swapaxes(shared_weights, 1, 2)
+    def load(*arrays):
+        return call(
+            load_kernel,
+            [shape(a.shape, a.dtype) for a in arrays],
+            "h" * len(arrays),
+            0,
+            sum(2 * a.size for a in arrays),
+            1,
+            [pltpu.SemaphoreType.DMA((len(arrays),))],
+        )(*arrays)
+
+    (gate_up,) = load(routed_gate_up[0])
+    down, shared_rows = load(routed_down[0], jnp.swapaxes(shared_weights, 1, 2))
     keeps, leaves, sums = [None] * steps, [None] * steps, []
     for chunk in chunks:
         blocks = [b for j in chunk for b in (direct[j], near[j])]
@@ -287,34 +297,26 @@
             "v" * count,
             4 * count * tok_rows * capacity * width,
             8 * count * capacity * width,
-            12,
+            8,
         )(*blocks)
         theirs = swap(theirs)
         shared = call(
             functools.partial(shared_kernel, count, width),
             shape((count * tok_rows, width), F32),
-            "v" * count + "h",
+            "v" * (count + 1),
             6 * count * tok_rows * width * shared_rows.shape[1],
             6 * width * shared_rows.shape[1],
-            24,
-            [pltpu.VMEM(shared_rows.shape, BF16), pltpu.SemaphoreType.DMA((3,))],
+            8,
         )(*blocks, shared_rows)
         sums += [x[count * capacity :][:count, :lanes] for x in (mine, theirs)]
-        parts = 4
         mine, theirs = call(
             expert_kernel,
             (results, results),
-            "vvhh",
+            "vvvv",
             12 * count * capacity * width * hidden_units,
             6 * width * hidden_units,
-            32,
-            [
-                pltpu.VMEM((2 * hidden_units // 128, width, 128), BF16),
-                pltpu.VMEM((parts, hidden_units, width // parts), BF16),
-                pltpu.VMEM((2 * count * capacity, hidden_units), BF16),
-                pltpu.SemaphoreType.DMA((2 * hidden_units // 128,)),
-                pltpu.SemaphoreType.DMA((parts,)),
-            ],
+            8,
+            [pltpu.VMEM((2 * count * capacity, hidden_units), BF16)],
         )(mine, theirs, gate_up, down)
         theirs = swap(theirs)
         tokens = (tok_rows, width)
@@ -324,7 +326,7 @@
             "v" * (count + 3),
             4 * count * tok_rows * capacity * width,
             8 * count * tok_rows * width,
-            16,
+            8,
         )(*blocks, mine, theirs, shared)
         for i, j in enumerate(chunk):
             keeps[j], leaves[j] = totals[2 * i], totals[2 * i + 1]
@@ -337,7 +339,12 @@
     mixed = mixed.astype(BF16)
 
     penalty = call(
-        functools.partial(penalty_kernel, all_experts, choose * float(all_tokens) * float(all_tokens)),
+        functools.partial(
+            penalty_kernel,
+            all_experts,
+            choose * float(all_tokens) * float(all_tokens),
+            [2 * j + b for chunk in chunks for j in chunk for b in range(2)],
+        ),
         shape((1, 1), F32),
         "v" * len(sums),
         0,

time: 123 us -> 106 us (0.86)
  waiting for transfers between devices: 61.2 us -> 48.8 us
  Pallas kernels: 34.3 us -> 26.5 us
  starting transfers between devices: 20 us -> 26.6 us
  local copies, waits for them, and re-layouts: 3.17 us -> 0.01 us
    ppermute x14, waiting for transfers between devices: 61.2 us -> 48.8 us  [cross(): lax.ppermute(block, 'expert', [(e, e ^ step) for e in range(expert_count)])]
    pallas_call x10 -> x12, Pallas kernels: 34.3 us -> 26.5 us  [go(): return run(*args)]
    ppermute x14, starting transfers between devices: 19.2 us -> 25.8 us  [cross(): lax.ppermute(block, 'expert', [(e, e ^ step) for e in range(expert_count)])]
    unnamed x8 -> x0, local copies, waits for them, and re-layouts: 3.16 us -> none
  transfers between devices with their start and end apart: 18 -> 18, of which waited for: 10 -> 10; matrix products, arithmetic and copies ran while one was open for 0% -> 0% of each run, Pallas kernels for 28% -> 24%
where the time goes in v1:
time: 106 us
  waiting for transfers between devices  48.8 us (46%)
  starting transfers between devices  26.6 us (25%)
  Pallas kernels  26.5 us (25%)
  between operations  2.61 us (2%)
    ppermute x14, waiting for transfers between devices, cross(): lax.ppermute(block, 'expert', [(e, e ^ step) for e in range(expert_count)])  48.8 us
    pallas_call x12, Pallas kernels, go(): return run(*args)  26.5 us
    ppermute x14, starting transfers between devices, cross(): lax.ppermute(block, 'expert', [(e, e ^ step) for e in range(expert_count)])  25.8 us
  transfers between devices with their start and end apart: 18, of which 10 were waited for; matrix products, arithmetic and copies ran while one was open for 0% of the time, Pallas kernels for 24%

profile of v1, /device:TPU:0, one launch (start us, length us, event | category | flops | bytes accessed | tf_op | source)
XLA Modules:
  0.0 105.6 jit_solution(7773605360896396685)
XLA Ops:
  1.3 1.6 %shard_map.95.refs_0_ = bf16[64,2176]{1,0:T(8,128)(2,1)S(1)} custom-call(s32[1]{0:T(128)S(6)} %copy.11.live_ref, bf16[64,2048]{1,0:T(8,128)(2,1)} %hidden_hbm.1, f32[1,2048]{1,0:T(1,128)} %bitcast.12, bf16[16,2048]{1,0:T(8,128)(2,1)} %bitcast.11, s32[6,64]{1,0:T(8,128)} %bitcast.13), custom_call_target="tpu_custom_call" | custom-call | flops 4194304 | bytes 524288 | tf_op jit(solution)/shard_map/pallas_call | solution.py:216
  2.9 4.1 %collective-permute-start.9 = (bf16[64,2176]{1,0:T(8,128)(2,1)S(1)}, bf16[64,2176]{1,0:T(8,128)(2,1)S(1)}, u32[]{:S(2)}, u32[]{:S(2)}) collective-permute-start(bf16[64,2176]{1,0:T(8,128)(2,1)S(1)} %shard_map.95.refs_0_), channel_id=1, source_target_pairs={{0,8},{2,10},{4,12},{6,14},{8,0},{10,2},{12,4},{14,6},{1,9},{3,11}... | collective-permute-start | bytes 835592 | tf_op jit(solution)/shard_map/ppermute | solution.py:248
  8.6 11.1 %collective-permute-done.9.refs_2_ = bf16[64,2176]{1,0:T(8,128)(2,1)S(1)} collective-permute-done((bf16[64,2176]{1,0:T(8,128)(2,1)S(1)}, bf16[64,2176]{1,0:T(8,128)(2,1)S(1)}, u32[]{:S(2)}, u32[]{:S(2)}) %collective-permute-start.9) | collective-permute-done | bytes 278560 | tf_op jit(solution)/shard_map/ppermute | solution.py:248
  19.7 1.6 %collective-permute-start.10 = (bf16[64,2176]{1,0:T(8,128)(2,1)S(1)}, bf16[64,2176]{1,0:T(8,128)(2,1)S(1)}, u32[]{:S(2)}, u32[]{:S(2)}) collective-permute-start(bf16[64,2176]{1,0:T(8,128)(2,1)S(1)} %collective-permute-done.9.refs_2_), channel_id=1, source_target_pairs={{0,2},{2,0},{4,6},{6,4},{8,10},{10,8},{12,14},{14,12},{1,3},{3,1},... | collective-permute-start | bytes 835592 | tf_op jit(solution)/shard_map/ppermute | solution.py:248
  21.2 3.5 %collective-permute-start.2 = (bf16[64,2176]{1,0:T(8,128)(2,1)S(1)}, bf16[64,2176]{1,0:T(8,128)(2,1)S(1)}, u32[]{:S(2)}, u32[]{:S(2)}) collective-permute-start(bf16[64,2176]{1,0:T(8,128)(2,1)S(1)} %shard_map.95.refs_0_), channel_id=1, source_target_pairs={{0,12},{2,14},{4,8},{6,10},{8,4},{10,6},{12,0},{14,2},{1,13},{3,15... | collective-permute-start | bytes 835592 | tf_op jit(solution)/shard_map/ppermute | solution.py:248
  24.7 2.8 %collective-permute-done.10.refs_3_ = bf16[64,2176]{1,0:T(8,128)(2,1)S(1)} collective-permute-done((bf16[64,2176]{1,0:T(8,128)(2,1)S(1)}, bf16[64,2176]{1,0:T(8,128)(2,1)S(1)}, u32[]{:S(2)}, u32[]{:S(2)}) %collective-permute-start.10) | collective-permute-done | bytes 278560 | tf_op jit(solution)/shard_map/ppermute | solution.py:248
  28.3 4.4 %collective-permute-done.2.refs_2_ = bf16[64,2176]{1,0:T(8,128)(2,1)S(1)} collective-permute-done((bf16[64,2176]{1,0:T(8,128)(2,1)S(1)}, bf16[64,2176]{1,0:T(8,128)(2,1)S(1)}, u32[]{:S(2)}, u32[]{:S(2)}) %collective-permute-start.2) | collective-permute-done | bytes 278560 | tf_op jit(solution)/shard_map/ppermute | solution.py:248
  33.1 4.3 %collective-permute-done.refs_0_ = bf16[64,2176]{1,0:T(8,128)(2,1)S(1)} collective-permute-done((bf16[64,2176]{1,0:T(8,128)(2,1)S(1)}, bf16[64,2176]{1,0:T(8,128)(2,1)S(1)}, u32[]{:S(2)}, u32[]{:S(2)}) %collective-permute-start) | collective-permute-done | bytes 278560 | tf_op jit(solution)/shard_map/ppermute | solution.py:248
  39.2 6.8 %collective-permute-done.1.refs_1_ = bf16[64,2176]{1,0:T(8,128)(2,1)S(1)} collective-permute-done((bf16[64,2176]{1,0:T(8,128)(2,1)S(1)}, bf16[64,2176]{1,0:T(8,128)(2,1)S(1)}, u32[]{:S(2)}, u32[]{:S(2)}) %collective-permute-start.1) | collective-permute-done | bytes 278560 | tf_op jit(solution)/shard_map/ppermute | solution.py:248
  46.7 4.3 %shard_map.97.up_ref = bf16[2048,2816]{1,0:T(8,128)(2,1)S(1)} custom-call(bf16[2048,2816]{1,0:T(8,128)(2,1)} %bitcast.8), custom_call_target="tpu_custom_call" | custom-call | bytes 11534336 | tf_op jit(solution)/shard_map/pallas_call | solution.py:216
  51.0 3.9 %shard_map.98 = (bf16[1408,2048]{1,0:T(8,128)(2,1)S(1)}, bf16[3,352,2048]{2,1,0:T(8,128)(2,1)S(1)}) custom-call(bf16[1408,2048]{1,0:T(8,128)(2,1)} %bitcast.9, bf16[3,352,2048]{2,1,0:T(8,128)(2,1)} %bitcast.10), custom_call_target="tpu_custom_call" | custom-call | bytes 10092544 | tf_op jit(solution)/shard_map/pallas_call | solution.py:216
  55.0 5.0 %shard_map.103 = (bf16[128,2048]{1,0:T(8,128)(2,1)S(1)}, bf16[128,2048]{1,0:T(8,128)(2,1)S(1)}) custom-call(bf16[144,2048]{1,0:T(8,128)(2,1)S(1)} %get-tuple-element.28.mine_ref, bf16[144,2048]{1,0:T(8,128)(2,1)S(1)} %collective-permute-done.11.peer_ref, bf16[2048,2816]{1,0:T(8,128)(2,1)S(1)} %shard_map.97.up_ref, ...), custom_call_target="tpu_custom_call" | custom-call | flops 4429185024 | bytes 17301504 | tf_op jit(solution)/shard_map/pallas_call | solution.py:216
  60.6 5.0 %shard_map.99 = (bf16[128,2048]{1,0:T(8,128)(2,1)S(1)}, bf16[128,2048]{1,0:T(8,128)(2,1)S(1)}) custom-call(bf16[144,2048]{1,0:T(8,128)(2,1)S(1)} %get-tuple-element.20.mine_ref, bf16[144,2048]{1,0:T(8,128)(2,1)S(1)} %collective-permute-done.4.peer_ref, bf16[2048,2816]{1,0:T(8,128)(2,1)S(1)} %shard_map.97.up_ref, ...), custom_call_target="tpu_custom_call" | custom-call | flops 4429185024 | bytes 17301504 | tf_op jit(solution)/shard_map/pallas_call | solution.py:216
  65.7 1.9 %shard_map.104.refs_6_ = f32[256,2048]{1,0:T(8,128)S(1)} custom-call(bf16[64,2176]{1,0:T(8,128)(2,1)S(1)} %shard_map.95.refs_0_, bf16[64,2176]{1,0:T(8,128)(2,1)S(1)} %collective-permute-done.8.refs_1_, bf16[64,2176]{1,0:T(8,128)(2,1)S(1)} %collective-permute-done.9.refs_2_, bf16[64,2176]{1,0:T(8,128)(2,1)S(1)} %collective-permute-done.10.refs_3_, ...), custom_call_target="tpu_custom_call" | custom-call | flops 1107296256 | bytes 4325376 | tf_op jit(solution)/shard_map/pallas_call | solution.py:216
  68.7 1.9 %shard_map.100.refs_6_ = f32[256,2048]{1,0:T(8,128)S(1)} custom-call(bf16[64,2176]{1,0:T(8,128)(2,1)S(1)} %collective-permute-done.refs_0_, bf16[64,2176]{1,0:T(8,128)(2,1)S(1)} %collective-permute-done.1.refs_1_, bf16[64,2176]{1,0:T(8,128)(2,1)S(1)} %collective-permute-done.2.refs_2_, bf16[64,2176]{1,0:T(8,128)(2,1)S(1)} %collective-permute-done.3.refs_3_, ...), custom_call_target="tpu_custom_call" | custom-call | flops 1107296256 | bytes 4325376 | tf_op jit(solution)/shard_map/pallas_call | solution.py:216
  70.6 1.6 %collective-permute-start.17 = (bf16[64,2048]{1,0:T(8,128)(2,1)S(1)}, bf16[64,2048]{1,0:T(8,128)(2,1)S(1)}, u32[]{:S(2)}, u32[]{:S(2)}) collective-permute-start(bf16[64,2048]{1,0:T(8,128)(2,1)S(1)} %get-tuple-element.37), channel_id=1, source_target_pairs={{0,2},{2,0},{4,6},{6,4},{8,10},{10,8},{12,14},{14,12},{1,3},{3,1},... | collective-permute-start | bytes 786440 | tf_op jit(solution)/shard_map/ppermute | solution.py:248
  73.3 1.5 %collective-permute-start.15 = (bf16[64,2048]{1,0:T(8,128)(2,1)S(1)}, bf16[64,2048]{1,0:T(8,128)(2,1)S(1)}, u32[]{:S(2)}, u32[]{:S(2)}) collective-permute-start(bf16[64,2048]{1,0:T(8,128)(2,1)S(1)} %get-tuple-element.35), channel_id=1, source_target_pairs={{0,2},{2,0},{4,6},{6,4},{8,10},{10,8},{12,14},{14,12},{1,3},{3,1},... | collective-permute-start | bytes 786440 | tf_op jit(solution)/shard_map/ppermute | solution.py:248
  74.8 2.6 %collective-permute-done.13 = bf16[64,2048]{1,0:T(8,128)(2,1)S(1)} collective-permute-done((bf16[64,2048]{1,0:T(8,128)(2,1)S(1)}, bf16[64,2048]{1,0:T(8,128)(2,1)S(1)}, u32[]{:S(2)}, u32[]{:S(2)}) %collective-permute-start.13) | collective-permute-done | bytes 262176 | tf_op jit(solution)/shard_map/ppermute | solution.py:248
  77.4 3.5 %collective-permute-start.14 = (bf16[64,2048]{1,0:T(8,128)(2,1)S(1)}, bf16[64,2048]{1,0:T(8,128)(2,1)S(1)}, u32[]{:S(2)}, u32[]{:S(2)}) collective-permute-start(bf16[64,2048]{1,0:T(8,128)(2,1)S(1)} %add_convert_fusion.2), channel_id=1, source_target_pairs={{0,8},{2,10},{4,12},{6,14},{8,0},{10,2},{12,4},{14,6},{1,9},{3,11}... | collective-permute-start | bytes 786440 | tf_op jit(solution)/shard_map/ppermute | solution.py:248
  80.9 7.7 %collective-permute-done.6 = bf16[64,2048]{1,0:T(8,128)(2,1)S(1)} collective-permute-done((bf16[64,2048]{1,0:T(8,128)(2,1)S(1)}, bf16[64,2048]{1,0:T(8,128)(2,1)S(1)}, u32[]{:S(2)}, u32[]{:S(2)}) %collective-permute-start.6) | collective-permute-done | bytes 262176 | tf_op jit(solution)/shard_map/ppermute | solution.py:248
  88.7 2.7 %collective-permute-start.7 = (bf16[64,2048]{1,0:T(8,128)(2,1)S(1)}, bf16[64,2048]{1,0:T(8,128)(2,1)S(1)}, u32[]{:S(2)}, u32[]{:S(2)}) collective-permute-start(bf16[64,2048]{1,0:T(8,128)(2,1)S(1)} %add_convert_fusion.3), channel_id=1, source_target_pairs={{0,12},{2,14},{4,8},{6,10},{8,4},{10,6},{12,0},{14,2},{1,13},{3,15... | collective-permute-start | bytes 786440 | tf_op jit(solution)/shard_map/ppermute | solution.py:248
  91.4 2.4 %collective-permute-done.15 = bf16[64,2048]{1,0:T(8,128)(2,1)S(1)} collective-permute-done((bf16[64,2048]{1,0:T(8,128)(2,1)S(1)}, bf16[64,2048]{1,0:T(8,128)(2,1)S(1)}, u32[]{:S(2)}, u32[]{:S(2)}) %collective-permute-start.15) | collective-permute-done | bytes 262176 | tf_op jit(solution)/shard_map/ppermute | solution.py:248
  93.8 3.7 %collective-permute-start.16 = (bf16[64,2048]{1,0:T(8,128)(2,1)S(1)}, bf16[64,2048]{1,0:T(8,128)(2,1)S(1)}, u32[]{:S(2)}, u32[]{:S(2)}) collective-permute-start(bf16[64,2048]{1,0:T(8,128)(2,1)S(1)} %add_convert_fusion.1), channel_id=1, source_target_pairs={{0,4},{2,6},{4,0},{6,2},{8,12},{10,14},{12,8},{14,10},{1,5},{3,7},... | collective-permute-start | bytes 786440 | tf_op jit(solution)/shard_map/ppermute | solution.py:248
  98.1 5.6 %collective-permute-done.16 = bf16[64,2048]{1,0:T(8,128)(2,1)S(1)} collective-permute-done((bf16[64,2048]{1,0:T(8,128)(2,1)S(1)}, bf16[64,2048]{1,0:T(8,128)(2,1)S(1)}, u32[]{:S(2)}, u32[]{:S(2)}) %collective-permute-start.16) | collective-permute-done | bytes 262176 | tf_op jit(solution)/shard_map/ppermute | solution.py:248
  (32 shorter events, 9.6 us)
Async XLA Ops:
  2.9 16.8 %collective-permute-start.9 = (bf16[64,2176]{1,0:T(8,128)(2,1)S(1)}, bf16[64,2176]{1,0:T(8,128)(2,1)S(1)}, u32[]{:S(2)}, u32[]{:S(2)}) collective-permute-start(bf16[64,2176]{1,0:T(8,128)(2,1)S(1)} %shard_map.95.refs_0_), channel_id=1, source_target_pairs={{0,8},{2,10},{4,12},{6,14},{8,0},{10,2},{12,4},{14,6},{1,9},{3,11}... | collective-permute-start | bytes 835592 | tf_op jit(solution)/shard_map/ppermute | solution.py:248
  7.0 17.7 %collective-permute-start.8 = (bf16[64,2176]{1,0:T(8,128)(2,1)S(1)}, bf16[64,2176]{1,0:T(8,128)(2,1)S(1)}, u32[]{:S(2)}, u32[]{:S(2)}) collective-permute-start(bf16[64,2176]{1,0:T(8,128)(2,1)S(1)} %shard_map.95.refs_0_), channel_id=1, source_target_pairs={{0,2},{2,0},{4,6},{6,4},{8,10},{10,8},{12,14},{14,12},{1,3},{3,1},... | collective-permute-start | bytes 835592 | tf_op jit(solution)/shard_map/ppermute | solution.py:248
  19.7 7.8 %collective-permute-start.10 = (bf16[64,2176]{1,0:T(8,128)(2,1)S(1)}, bf16[64,2176]{1,0:T(8,128)(2,1)S(1)}, u32[]{:S(2)}, u32[]{:S(2)}) collective-permute-start(bf16[64,2176]{1,0:T(8,128)(2,1)S(1)} %collective-permute-done.9.refs_2_), channel_id=1, source_target_pairs={{0,2},{2,0},{4,6},{6,4},{8,10},{10,8},{12,14},{14,12},{1,3},{3,1},... | collective-permute-start | bytes 835592 | tf_op jit(solution)/shard_map/ppermute | solution.py:248
  21.2 11.4 %collective-permute-start.2 = (bf16[64,2176]{1,0:T(8,128)(2,1)S(1)}, bf16[64,2176]{1,0:T(8,128)(2,1)S(1)}, u32[]{:S(2)}, u32[]{:S(2)}) collective-permute-start(bf16[64,2176]{1,0:T(8,128)(2,1)S(1)} %shard_map.95.refs_0_), channel_id=1, source_target_pairs={{0,12},{2,14},{4,8},{6,10},{8,4},{10,6},{12,0},{14,2},{1,13},{3,15... | collective-permute-start | bytes 835592 | tf_op jit(solution)/shard_map/ppermute | solution.py:248
  24.7 12.6 %collective-permute-start = (bf16[64,2176]{1,0:T(8,128)(2,1)S(1)}, bf16[64,2176]{1,0:T(8,128)(2,1)S(1)}, u32[]{:S(2)}, u32[]{:S(2)}) collective-permute-start(bf16[64,2176]{1,0:T(8,128)(2,1)S(1)} %shard_map.95.refs_0_), channel_id=1, source_target_pairs={{0,4},{2,6},{4,0},{6,2},{8,12},{10,14},{12,8},{14,10},{1,5},{3,7},... | collective-permute-start | bytes 835592 | tf_op jit(solution)/shard_map/ppermute | solution.py:248
  28.2 26.8 %collective-permute-start.11 = (bf16[144,2048]{1,0:T(8,128)(2,1)S(1)}, bf16[144,2048]{1,0:T(8,128)(2,1)S(1)}, u32[]{:S(2)}, u32[]{:S(2)}) collective-permute-start(bf16[144,2048]{1,0:T(8,128)(2,1)S(1)} %get-tuple-element.29), channel_id=1, source_target_pairs={{0,1},{1,0},{2,3},{3,2},{4,5},{5,4},{6,7},{7,6},{8,9},{9,8},{10,11... | collective-permute-start | bytes 1769480 | tf_op jit(solution)/shard_map/ppermute | solution.py:251
  32.6 6.5 %collective-permute-start.3 = (bf16[64,2176]{1,0:T(8,128)(2,1)S(1)}, bf16[64,2176]{1,0:T(8,128)(2,1)S(1)}, u32[]{:S(2)}, u32[]{:S(2)}) collective-permute-start(bf16[64,2176]{1,0:T(8,128)(2,1)S(1)} %collective-permute-done.2.refs_2_), channel_id=1, source_target_pairs={{0,2},{2,0},{4,6},{6,4},{8,10},{10,8},{12,14},{14,12},{1,3},{3,1},... | collective-permute-start | bytes 835592 | tf_op jit(solution)/shard_map/ppermute | solution.py:248
  37.4 8.6 %collective-permute-start.1 = (bf16[64,2176]{1,0:T(8,128)(2,1)S(1)}, bf16[64,2176]{1,0:T(8,128)(2,1)S(1)}, u32[]{:S(2)}, u32[]{:S(2)}) collective-permute-start(bf16[64,2176]{1,0:T(8,128)(2,1)S(1)} %collective-permute-done.refs_0_), channel_id=1, source_target_pairs={{0,2},{2,0},{4,6},{6,4},{8,10},{10,8},{12,14},{14,12},{1,3},{3,1},... | collective-permute-start | bytes 835592 | tf_op jit(solution)/shard_map/ppermute | solution.py:248
  46.6 14.0 %collective-permute-start.4 = (bf16[144,2048]{1,0:T(8,128)(2,1)S(1)}, bf16[144,2048]{1,0:T(8,128)(2,1)S(1)}, u32[]{:S(2)}, u32[]{:S(2)}) collective-permute-start(bf16[144,2048]{1,0:T(8,128)(2,1)S(1)} %get-tuple-element.21), channel_id=1, source_target_pairs={{0,1},{1,0},{2,3},{3,2},{4,5},{5,4},{6,7},{7,6},{8,9},{9,8},{10,11... | collective-permute-start | bytes 1769480 | tf_op jit(solution)/shard_map/ppermute | solution.py:251
  60.0 7.6 %collective-permute-start.12 = (bf16[128,2048]{1,0:T(8,128)(2,1)S(1)}, bf16[128,2048]{1,0:T(8,128)(2,1)S(1)}, u32[]{:S(2)}, u32[]{:S(2)}) collective-permute-start(bf16[128,2048]{1,0:T(8,128)(2,1)S(1)} %get-tuple-element.31), channel_id=1, source_target_pairs={{0,1},{1,0},{2,3},{3,2},{4,5},{5,4},{6,7},{7,6},{8,9},{9,8},{10,11... | collective-permute-start | bytes 1572872 | tf_op jit(solution)/shard_map/ppermute | solution.py:251
  65.6 6.5 %collective-permute-start.5 = (bf16[128,2048]{1,0:T(8,128)(2,1)S(1)}, bf16[128,2048]{1,0:T(8,128)(2,1)S(1)}, u32[]{:S(2)}, u32[]{:S(2)}) collective-permute-start(bf16[128,2048]{1,0:T(8,128)(2,1)S(1)} %get-tuple-element.24), channel_id=1, source_target_pairs={{0,1},{1,0},{2,3},{3,2},{4,5},{5,4},{6,7},{7,6},{8,9},{9,8},{10,11... | collective-permute-start | bytes 1572872 | tf_op jit(solution)/shard_map/ppermute | solution.py:251
  68.1 9.2 %collective-permute-start.13 = (bf16[64,2048]{1,0:T(8,128)(2,1)S(1)}, bf16[64,2048]{1,0:T(8,128)(2,1)S(1)}, u32[]{:S(2)}, u32[]{:S(2)}) collective-permute-start(bf16[64,2048]{1,0:T(8,128)(2,1)S(1)} %get-tuple-element.33), channel_id=1, source_target_pairs={{0,2},{2,0},{4,6},{6,4},{8,10},{10,8},{12,14},{14,12},{1,3},{3,1},... | collective-permute-start | bytes 786440 | tf_op jit(solution)/shard_map/ppermute | solution.py:248
  70.6 27.4 %collective-permute-start.17 = (bf16[64,2048]{1,0:T(8,128)(2,1)S(1)}, bf16[64,2048]{1,0:T(8,128)(2,1)S(1)}, u32[]{:S(2)}, u32[]{:S(2)}) collective-permute-start(bf16[64,2048]{1,0:T(8,128)(2,1)S(1)} %get-tuple-element.37), channel_id=1, source_target_pairs={{0,2},{2,0},{4,6},{6,4},{8,10},{10,8},{12,14},{14,12},{1,3},{3,1},... | collective-permute-start | bytes 786440 | tf_op jit(solution)/shard_map/ppermute | solution.py:248
  72.7 15.9 %collective-permute-start.6 = (bf16[64,2048]{1,0:T(8,128)(2,1)S(1)}, bf16[64,2048]{1,0:T(8,128)(2,1)S(1)}, u32[]{:S(2)}, u32[]{:S(2)}) collective-permute-start(bf16[64,2048]{1,0:T(8,128)(2,1)S(1)} %get-tuple-element.27), channel_id=1, source_target_pairs={{0,2},{2,0},{4,6},{6,4},{8,10},{10,8},{12,14},{14,12},{1,3},{3,1},... | collective-permute-start | bytes 786440 | tf_op jit(solution)/shard_map/ppermute | solution.py:248
  73.3 20.5 %collective-permute-start.15 = (bf16[64,2048]{1,0:T(8,128)(2,1)S(1)}, bf16[64,2048]{1,0:T(8,128)(2,1)S(1)}, u32[]{:S(2)}, u32[]{:S(2)}) collective-permute-start(bf16[64,2048]{1,0:T(8,128)(2,1)S(1)} %get-tuple-element.35), channel_id=1, source_target_pairs={{0,2},{2,0},{4,6},{6,4},{8,10},{10,8},{12,14},{14,12},{1,3},{3,1},... | collective-permute-start | bytes 786440 | tf_op jit(solution)/shard_map/ppermute | solution.py:248
  77.4 20.6 %collective-permute-start.14 = (bf16[64,2048]{1,0:T(8,128)(2,1)S(1)}, bf16[64,2048]{1,0:T(8,128)(2,1)S(1)}, u32[]{:S(2)}, u32[]{:S(2)}) collective-permute-start(bf16[64,2048]{1,0:T(8,128)(2,1)S(1)} %add_convert_fusion.2), channel_id=1, source_target_pairs={{0,8},{2,10},{4,12},{6,14},{8,0},{10,2},{12,4},{14,6},{1,9},{3,11}... | collective-permute-start | bytes 786440 | tf_op jit(solution)/shard_map/ppermute | solution.py:248
  88.7 9.4 %collective-permute-start.7 = (bf16[64,2048]{1,0:T(8,128)(2,1)S(1)}, bf16[64,2048]{1,0:T(8,128)(2,1)S(1)}, u32[]{:S(2)}, u32[]{:S(2)}) collective-permute-start(bf16[64,2048]{1,0:T(8,128)(2,1)S(1)} %add_convert_fusion.3), channel_id=1, source_target_pairs={{0,12},{2,14},{4,8},{6,10},{8,4},{10,6},{12,0},{14,2},{1,13},{3,15... | collective-permute-start | bytes 786440 | tf_op jit(solution)/shard_map/ppermute | solution.py:248
  93.8 9.8 %collective-permute-start.16 = (bf16[64,2048]{1,0:T(8,128)(2,1)S(1)}, bf16[64,2048]{1,0:T(8,128)(2,1)S(1)}, u32[]{:S(2)}, u32[]{:S(2)}) collective-permute-start(bf16[64,2048]{1,0:T(8,128)(2,1)S(1)} %add_convert_fusion.1), channel_id=1, source_target_pairs={{0,4},{2,6},{4,0},{6,2},{8,12},{10,14},{12,8},{14,10},{1,5},{3,7},... | collective-permute-start | bytes 786440 | tf_op jit(solution)/shard_map/ppermute | solution.py:248

commit v2 on v1

--- a/solution.py
+++ b/solution.py
@@ -32,8 +32,15 @@
     return me, me ^ 1
 
 
-def route_kernel(live_ref, hidden_hbm, gain_hbm, router_hbm, ids_hbm, packet_ref, hidden_ref, gain_ref, router_ref, ids_ref, sems):
-    pairs = ((hidden_hbm, hidden_ref), (gain_hbm, gain_ref), (router_hbm, router_ref), (ids_hbm, ids_ref))
+def route_kernel(
+    live_ref, hidden_hbm, gain_hbm, router_hbm, ids_hbm, packet_ref, hidden_ref, gain_ref, router_ref, ids_ref, sems
+):
+    pairs = (
+        (hidden_hbm, hidden_ref),
+        (gain_hbm, gain_ref),
+        (router_hbm, router_ref),
+        (ids_hbm, ids_ref),
+    )
     copies = [pltpu.make_async_copy(x, y, sems.at[i]) for i, (x, y) in enumerate(pairs)]
     for c in copies:
         c.start()
@@ -269,7 +276,9 @@
 
     steps = expert_count // 2
     chunks = chunks_of(steps)
-    direct = [packet] + [cross(packet, 2 * j) for j in range(1, steps)]
+    direct = [packet, cross(packet, 2)]
+    for j in range(2, steps):
+        direct.append(cross(direct[j - 1], 2) if j % 2 else cross(packet, 2 * j))
     near = [cross(direct[j], 1) for j in range(steps)]
 
     def load(*arrays):

time: 106 us -> 104 us (0.981)
  starting transfers between devices: 26.6 us -> 23.5 us
  waiting for transfers between devices: 48.8 us -> 50.1 us
    ppermute x14, starting transfers between devices: 25.8 us -> 22.7 us  [cross(): lax.ppermute(block, 'expert', [(e, e ^ step) for e in range(expert_count)])]
    ppermute x14, waiting for transfers between devices: 48.8 us -> 50.1 us  [cross(): lax.ppermute(block, 'expert', [(e, e ^ step) for e in range(expert_count)])]
  transfers between devices with their start and end apart: 18 -> 18, of which waited for: 10 -> 11; matrix products, arithmetic and copies ran while one was open for 0% -> 0% of each run, Pallas kernels for 24% -> 24%
where the time goes in v2:
time: 104 us
  waiting for transfers between devices  50.1 us (48%)
  Pallas kernels  26.5 us (25%)
  starting transfers between devices  23.5 us (23%)
  between operations  2.61 us (3%)
    ppermute x14, waiting for transfers between devices, cross(): lax.ppermute(block, 'expert', [(e, e ^ step) for e in range(expert_count)])  50.1 us
    pallas_call x12, Pallas kernels, go(): return run(*args)  26.5 us
    ppermute x14, starting transfers between devices, cross(): lax.ppermute(block, 'expert', [(e, e ^ step) for e in range(expert_count)])  22.7 us
  transfers between devices with their start and end apart: 18, of which 11 were waited for; matrix products, arithmetic and copies ran while one was open for 0% of the time, Pallas kernels for 24%

profile of v2, /device:TPU:0, one launch (start us, length us, event | category | flops | bytes accessed | tf_op | source)
XLA Modules:
  0.0 103.7 jit_solution(3676143761886121278)
XLA Ops:
  1.3 1.6 %shard_map.95.refs_0_ = bf16[64,2176]{1,0:T(8,128)(2,1)S(1)} custom-call(s32[1]{0:T(128)S(6)} %copy.11.live_ref, bf16[64,2048]{1,0:T(8,128)(2,1)} %hidden_hbm.1, f32[1,2048]{1,0:T(1,128)} %bitcast.12, bf16[16,2048]{1,0:T(8,128)(2,1)} %bitcast.11, s32[6,64]{1,0:T(8,128)} %bitcast.13), custom_call_target="tpu_custom_call" | custom-call | flops 4194304 | bytes 524288 | tf_op jit(solution)/shard_map/pallas_call | solution.py:223
  2.9 4.1 %collective-permute-start.2 = (bf16[64,2176]{1,0:T(8,128)(2,1)S(1)}, bf16[64,2176]{1,0:T(8,128)(2,1)S(1)}, u32[]{:S(2)}, u32[]{:S(2)}) collective-permute-start(bf16[64,2176]{1,0:T(8,128)(2,1)S(1)} %shard_map.95.refs_0_), channel_id=1, source_target_pairs={{0,8},{2,10},{4,12},{6,14},{8,0},{10,2},{12,4},{14,6},{1,9},{3,11}... | collective-permute-start | bytes 835592 | tf_op jit(solution)/shard_map/ppermute | solution.py:255
  7.0 1.5 %collective-permute-start.9 = (bf16[64,2176]{1,0:T(8,128)(2,1)S(1)}, bf16[64,2176]{1,0:T(8,128)(2,1)S(1)}, u32[]{:S(2)}, u32[]{:S(2)}) collective-permute-start(bf16[64,2176]{1,0:T(8,128)(2,1)S(1)} %shard_map.95.refs_0_), channel_id=1, source_target_pairs={{0,2},{2,0},{4,6},{6,4},{8,10},{10,8},{12,14},{14,12},{1,3},{3,1},... | collective-permute-start | bytes 835592 | tf_op jit(solution)/shard_map/ppermute | solution.py:255
  8.6 11.1 %collective-permute-done.2.refs_2_ = bf16[64,2176]{1,0:T(8,128)(2,1)S(1)} collective-permute-done((bf16[64,2176]{1,0:T(8,128)(2,1)S(1)}, bf16[64,2176]{1,0:T(8,128)(2,1)S(1)}, u32[]{:S(2)}, u32[]{:S(2)}) %collective-permute-start.2) | collective-permute-done | bytes 278560 | tf_op jit(solution)/shard_map/ppermute | solution.py:255
  19.7 1.6 %collective-permute-start.10 = (bf16[64,2176]{1,0:T(8,128)(2,1)S(1)}, bf16[64,2176]{1,0:T(8,128)(2,1)S(1)}, u32[]{:S(2)}, u32[]{:S(2)}) collective-permute-start(bf16[64,2176]{1,0:T(8,128)(2,1)S(1)} %collective-permute-done.2.refs_2_), channel_id=1, source_target_pairs={{0,2},{2,0},{4,6},{6,4},{8,10},{10,8},{12,14},{14,12},{1,3},{3,1},... | collective-permute-start | bytes 835592 | tf_op jit(solution)/shard_map/ppermute | solution.py:255
  23.3 4.2 %collective-permute-done.10.refs_3_ = bf16[64,2176]{1,0:T(8,128)(2,1)S(1)} collective-permute-done((bf16[64,2176]{1,0:T(8,128)(2,1)S(1)}, bf16[64,2176]{1,0:T(8,128)(2,1)S(1)}, u32[]{:S(2)}, u32[]{:S(2)}) %collective-permute-start.10) | collective-permute-done | bytes 278560 | tf_op jit(solution)/shard_map/ppermute | solution.py:255
  28.3 2.5 %collective-permute-done.refs_0_ = bf16[64,2176]{1,0:T(8,128)(2,1)S(1)} collective-permute-done((bf16[64,2176]{1,0:T(8,128)(2,1)S(1)}, bf16[64,2176]{1,0:T(8,128)(2,1)S(1)}, u32[]{:S(2)}, u32[]{:S(2)}) %collective-permute-start) | collective-permute-done | bytes 278560 | tf_op jit(solution)/shard_map/ppermute | solution.py:255
  31.2 3.3 %collective-permute-done.3.refs_2_ = bf16[64,2176]{1,0:T(8,128)(2,1)S(1)} collective-permute-done((bf16[64,2176]{1,0:T(8,128)(2,1)S(1)}, bf16[64,2176]{1,0:T(8,128)(2,1)S(1)}, u32[]{:S(2)}, u32[]{:S(2)}) %collective-permute-start.3) | collective-permute-done | bytes 278560 | tf_op jit(solution)/shard_map/ppermute | solution.py:255
  35.2 4.2 %collective-permute-done.1.refs_1_ = bf16[64,2176]{1,0:T(8,128)(2,1)S(1)} collective-permute-done((bf16[64,2176]{1,0:T(8,128)(2,1)S(1)}, bf16[64,2176]{1,0:T(8,128)(2,1)S(1)}, u32[]{:S(2)}, u32[]{:S(2)}) %collective-permute-start.1) | collective-permute-done | bytes 278560 | tf_op jit(solution)/shard_map/ppermute | solution.py:255
  39.5 3.8 %collective-permute-done.4.refs_3_ = bf16[64,2176]{1,0:T(8,128)(2,1)S(1)} collective-permute-done((bf16[64,2176]{1,0:T(8,128)(2,1)S(1)}, bf16[64,2176]{1,0:T(8,128)(2,1)S(1)}, u32[]{:S(2)}, u32[]{:S(2)}) %collective-permute-start.4) | collective-permute-done | bytes 278560 | tf_op jit(solution)/shard_map/ppermute | solution.py:255
  44.0 4.3 %shard_map.97.up_ref = bf16[2048,2816]{1,0:T(8,128)(2,1)S(1)} custom-call(bf16[2048,2816]{1,0:T(8,128)(2,1)} %bitcast.8), custom_call_target="tpu_custom_call" | custom-call | bytes 11534336 | tf_op jit(solution)/shard_map/pallas_call | solution.py:223
  48.3 3.9 %shard_map.98 = (bf16[1408,2048]{1,0:T(8,128)(2,1)S(1)}, bf16[3,352,2048]{2,1,0:T(8,128)(2,1)S(1)}) custom-call(bf16[1408,2048]{1,0:T(8,128)(2,1)} %bitcast.9, bf16[3,352,2048]{2,1,0:T(8,128)(2,1)} %bitcast.10), custom_call_target="tpu_custom_call" | custom-call | bytes 10092544 | tf_op jit(solution)/shard_map/pallas_call | solution.py:223
  52.3 5.0 %shard_map.103 = (bf16[128,2048]{1,0:T(8,128)(2,1)S(1)}, bf16[128,2048]{1,0:T(8,128)(2,1)S(1)}) custom-call(bf16[144,2048]{1,0:T(8,128)(2,1)S(1)} %get-tuple-element.28.mine_ref, bf16[144,2048]{1,0:T(8,128)(2,1)S(1)} %collective-permute-done.11.peer_ref, bf16[2048,2816]{1,0:T(8,128)(2,1)S(1)} %shard_map.97.up_ref, ...), custom_call_target="tpu_custom_call" | custom-call | flops 4429185024 | bytes 17301504 | tf_op jit(solution)/shard_map/pallas_call | solution.py:223
  57.9 5.0 %shard_map.99 = (bf16[128,2048]{1,0:T(8,128)(2,1)S(1)}, bf16[128,2048]{1,0:T(8,128)(2,1)S(1)}) custom-call(bf16[144,2048]{1,0:T(8,128)(2,1)S(1)} %get-tuple-element.20.mine_ref, bf16[144,2048]{1,0:T(8,128)(2,1)S(1)} %collective-permute-done.5.peer_ref, bf16[2048,2816]{1,0:T(8,128)(2,1)S(1)} %shard_map.97.up_ref, ...), custom_call_target="tpu_custom_call" | custom-call | flops 4429185024 | bytes 17301504 | tf_op jit(solution)/shard_map/pallas_call | solution.py:223
  63.1 1.9 %shard_map.104.refs_6_ = f32[256,2048]{1,0:T(8,128)S(1)} custom-call(bf16[64,2176]{1,0:T(8,128)(2,1)S(1)} %shard_map.95.refs_0_, bf16[64,2176]{1,0:T(8,128)(2,1)S(1)} %collective-permute-done.9.refs_1_, bf16[64,2176]{1,0:T(8,128)(2,1)S(1)} %collective-permute-done.2.refs_2_, bf16[64,2176]{1,0:T(8,128)(2,1)S(1)} %collective-permute-done.10.refs_3_, ...), custom_call_target="tpu_custom_call" | custom-call | flops 1107296256 | bytes 4325376 | tf_op jit(solution)/shard_map/pallas_call | solution.py:223
  65.5 1.4 %collective-permute-start.13 = (bf16[64,2048]{1,0:T(8,128)(2,1)S(1)}, bf16[64,2048]{1,0:T(8,128)(2,1)S(1)}, u32[]{:S(2)}, u32[]{:S(2)}) collective-permute-start(bf16[64,2048]{1,0:T(8,128)(2,1)S(1)} %get-tuple-element.33), channel_id=1, source_target_pairs={{0,2},{2,0},{4,6},{6,4},{8,10},{10,8},{12,14},{14,12},{1,3},{3,1},... | collective-permute-start | bytes 786440 | tf_op jit(solution)/shard_map/ppermute | solution.py:255
  66.9 1.9 %shard_map.100.refs_6_ = f32[256,2048]{1,0:T(8,128)S(1)} custom-call(bf16[64,2176]{1,0:T(8,128)(2,1)S(1)} %collective-permute-done.refs_0_, bf16[64,2176]{1,0:T(8,128)(2,1)S(1)} %collective-permute-done.1.refs_1_, bf16[64,2176]{1,0:T(8,128)(2,1)S(1)} %collective-permute-done.3.refs_2_, bf16[64,2176]{1,0:T(8,128)(2,1)S(1)} %collective-permute-done.4.refs_3_, ...), custom_call_target="tpu_custom_call" | custom-call | flops 1107296256 | bytes 4325376 | tf_op jit(solution)/shard_map/pallas_call | solution.py:223
  71.4 3.3 %collective-permute-done.13 = bf16[64,2048]{1,0:T(8,128)(2,1)S(1)} collective-permute-done((bf16[64,2048]{1,0:T(8,128)(2,1)S(1)}, bf16[64,2048]{1,0:T(8,128)(2,1)S(1)}, u32[]{:S(2)}, u32[]{:S(2)}) %collective-permute-start.13) | collective-permute-done | bytes 262176 | tf_op jit(solution)/shard_map/ppermute | solution.py:255
  74.8 2.3 %collective-permute-start.14 = (bf16[64,2048]{1,0:T(8,128)(2,1)S(1)}, bf16[64,2048]{1,0:T(8,128)(2,1)S(1)}, u32[]{:S(2)}, u32[]{:S(2)}) collective-permute-start(bf16[64,2048]{1,0:T(8,128)(2,1)S(1)} %add_convert_fusion.2), channel_id=1, source_target_pairs={{0,8},{2,10},{4,12},{6,14},{8,0},{10,2},{12,4},{14,6},{1,9},{3,11}... | collective-permute-start | bytes 786440 | tf_op jit(solution)/shard_map/ppermute | solution.py:255
  77.6 8.3 %collective-permute-done.7 = bf16[64,2048]{1,0:T(8,128)(2,1)S(1)} collective-permute-done((bf16[64,2048]{1,0:T(8,128)(2,1)S(1)}, bf16[64,2048]{1,0:T(8,128)(2,1)S(1)}, u32[]{:S(2)}, u32[]{:S(2)}) %collective-permute-start.7) | collective-permute-done | bytes 262176 | tf_op jit(solution)/shard_map/ppermute | solution.py:255
  86.0 4.4 %collective-permute-start.8 = (bf16[64,2048]{1,0:T(8,128)(2,1)S(1)}, bf16[64,2048]{1,0:T(8,128)(2,1)S(1)}, u32[]{:S(2)}, u32[]{:S(2)}) collective-permute-start(bf16[64,2048]{1,0:T(8,128)(2,1)S(1)} %add_convert_fusion.3), channel_id=1, source_target_pairs={{0,12},{2,14},{4,8},{6,10},{8,4},{10,6},{12,0},{14,2},{1,13},{3,15... | collective-permute-start | bytes 786440 | tf_op jit(solution)/shard_map/ppermute | solution.py:255
  91.2 1.6 %collective-permute-start.16 = (bf16[64,2048]{1,0:T(8,128)(2,1)S(1)}, bf16[64,2048]{1,0:T(8,128)(2,1)S(1)}, u32[]{:S(2)}, u32[]{:S(2)}) collective-permute-start(bf16[64,2048]{1,0:T(8,128)(2,1)S(1)} %add_convert_fusion.1), channel_id=1, source_target_pairs={{0,4},{2,6},{4,0},{6,2},{8,12},{10,14},{12,8},{14,10},{1,5},{3,7},... | collective-permute-start | bytes 786440 | tf_op jit(solution)/shard_map/ppermute | solution.py:255
  93.2 3.9 %collective-permute-done.8 = bf16[64,2048]{1,0:T(8,128)(2,1)S(1)} collective-permute-done((bf16[64,2048]{1,0:T(8,128)(2,1)S(1)}, bf16[64,2048]{1,0:T(8,128)(2,1)S(1)}, u32[]{:S(2)}, u32[]{:S(2)}) %collective-permute-start.8) | collective-permute-done | bytes 262176 | tf_op jit(solution)/shard_map/ppermute | solution.py:255
  97.1 4.7 %collective-permute-done.16 = bf16[64,2048]{1,0:T(8,128)(2,1)S(1)} collective-permute-done((bf16[64,2048]{1,0:T(8,128)(2,1)S(1)}, bf16[64,2048]{1,0:T(8,128)(2,1)S(1)}, u32[]{:S(2)}, u32[]{:S(2)}) %collective-permute-start.16) | collective-permute-done | bytes 262176 | tf_op jit(solution)/shard_map/ppermute | solution.py:255
  (32 shorter events, 11.2 us)
Async XLA Ops:
  2.9 16.8 %collective-permute-start.2 = (bf16[64,2176]{1,0:T(8,128)(2,1)S(1)}, bf16[64,2176]{1,0:T(8,128)(2,1)S(1)}, u32[]{:S(2)}, u32[]{:S(2)}) collective-permute-start(bf16[64,2176]{1,0:T(8,128)(2,1)S(1)} %shard_map.95.refs_0_), channel_id=1, source_target_pairs={{0,8},{2,10},{4,12},{6,14},{8,0},{10,2},{12,4},{14,6},{1,9},{3,11}... | collective-permute-start | bytes 835592 | tf_op jit(solution)/shard_map/ppermute | solution.py:255
  7.0 16.2 %collective-permute-start.9 = (bf16[64,2176]{1,0:T(8,128)(2,1)S(1)}, bf16[64,2176]{1,0:T(8,128)(2,1)S(1)}, u32[]{:S(2)}, u32[]{:S(2)}) collective-permute-start(bf16[64,2176]{1,0:T(8,128)(2,1)S(1)} %shard_map.95.refs_0_), channel_id=1, source_target_pairs={{0,2},{2,0},{4,6},{6,4},{8,10},{10,8},{12,14},{14,12},{1,3},{3,1},... | collective-permute-start | bytes 835592 | tf_op jit(solution)/shard_map/ppermute | solution.py:255
  19.7 7.8 %collective-permute-start.10 = (bf16[64,2176]{1,0:T(8,128)(2,1)S(1)}, bf16[64,2176]{1,0:T(8,128)(2,1)S(1)}, u32[]{:S(2)}, u32[]{:S(2)}) collective-permute-start(bf16[64,2176]{1,0:T(8,128)(2,1)S(1)} %collective-permute-done.2.refs_2_), channel_id=1, source_target_pairs={{0,2},{2,0},{4,6},{6,4},{8,10},{10,8},{12,14},{14,12},{1,3},{3,1},... | collective-permute-start | bytes 835592 | tf_op jit(solution)/shard_map/ppermute | solution.py:255
  21.2 9.5 %collective-permute-start = (bf16[64,2176]{1,0:T(8,128)(2,1)S(1)}, bf16[64,2176]{1,0:T(8,128)(2,1)S(1)}, u32[]{:S(2)}, u32[]{:S(2)}) collective-permute-start(bf16[64,2176]{1,0:T(8,128)(2,1)S(1)} %shard_map.95.refs_0_), channel_id=1, source_target_pairs={{0,4},{2,6},{4,0},{6,2},{8,12},{10,14},{12,8},{14,10},{1,5},{3,7},... | collective-permute-start | bytes 835592 | tf_op jit(solution)/shard_map/ppermute | solution.py:255
  21.9 12.6 %collective-permute-start.3 = (bf16[64,2176]{1,0:T(8,128)(2,1)S(1)}, bf16[64,2176]{1,0:T(8,128)(2,1)S(1)}, u32[]{:S(2)}, u32[]{:S(2)}) collective-permute-start(bf16[64,2176]{1,0:T(8,128)(2,1)S(1)} %collective-permute-done.2.refs_2_), channel_id=1, source_target_pairs={{0,4},{2,6},{4,0},{6,2},{8,12},{10,14},{12,8},{14,10},{1,5},{3,7},... | collective-permute-start | bytes 835592 | tf_op jit(solution)/shard_map/ppermute | solution.py:255
  28.2 24.1 %collective-permute-start.11 = (bf16[144,2048]{1,0:T(8,128)(2,1)S(1)}, bf16[144,2048]{1,0:T(8,128)(2,1)S(1)}, u32[]{:S(2)}, u32[]{:S(2)}) collective-permute-start(bf16[144,2048]{1,0:T(8,128)(2,1)S(1)} %get-tuple-element.29), channel_id=1, source_target_pairs={{0,1},{1,0},{2,3},{3,2},{4,5},{5,4},{6,7},{7,6},{8,9},{9,8},{10,11... | collective-permute-start | bytes 1769480 | tf_op jit(solution)/shard_map/ppermute | solution.py:258
  30.8 8.7 %collective-permute-start.1 = (bf16[64,2176]{1,0:T(8,128)(2,1)S(1)}, bf16[64,2176]{1,0:T(8,128)(2,1)S(1)}, u32[]{:S(2)}, u32[]{:S(2)}) collective-permute-start(bf16[64,2176]{1,0:T(8,128)(2,1)S(1)} %collective-permute-done.refs_0_), channel_id=1, source_target_pairs={{0,2},{2,0},{4,6},{6,4},{8,10},{10,8},{12,14},{14,12},{1,3},{3,1},... | collective-permute-start | bytes 835592 | tf_op jit(solution)/shard_map/ppermute | solution.py:255
  34.5 8.8 %collective-permute-start.4 = (bf16[64,2176]{1,0:T(8,128)(2,1)S(1)}, bf16[64,2176]{1,0:T(8,128)(2,1)S(1)}, u32[]{:S(2)}, u32[]{:S(2)}) collective-permute-start(bf16[64,2176]{1,0:T(8,128)(2,1)S(1)} %collective-permute-done.3.refs_2_), channel_id=1, source_target_pairs={{0,2},{2,0},{4,6},{6,4},{8,10},{10,8},{12,14},{14,12},{1,3},{3,1},... | collective-permute-start | bytes 835592 | tf_op jit(solution)/shard_map/ppermute | solution.py:255
  44.0 14.0 %collective-permute-start.5 = (bf16[144,2048]{1,0:T(8,128)(2,1)S(1)}, bf16[144,2048]{1,0:T(8,128)(2,1)S(1)}, u32[]{:S(2)}, u32[]{:S(2)}) collective-permute-start(bf16[144,2048]{1,0:T(8,128)(2,1)S(1)} %get-tuple-element.21), channel_id=1, source_target_pairs={{0,1},{1,0},{2,3},{3,2},{4,5},{5,4},{6,7},{7,6},{8,9},{9,8},{10,11... | collective-permute-start | bytes 1769480 | tf_op jit(solution)/shard_map/ppermute | solution.py:258
  57.4 7.6 %collective-permute-start.12 = (bf16[128,2048]{1,0:T(8,128)(2,1)S(1)}, bf16[128,2048]{1,0:T(8,128)(2,1)S(1)}, u32[]{:S(2)}, u32[]{:S(2)}) collective-permute-start(bf16[128,2048]{1,0:T(8,128)(2,1)S(1)} %get-tuple-element.31), channel_id=1, source_target_pairs={{0,1},{1,0},{2,3},{3,2},{4,5},{5,4},{6,7},{7,6},{8,9},{9,8},{10,11... | collective-permute-start | bytes 1572872 | tf_op jit(solution)/shard_map/ppermute | solution.py:258
  63.0 6.5 %collective-permute-start.6 = (bf16[128,2048]{1,0:T(8,128)(2,1)S(1)}, bf16[128,2048]{1,0:T(8,128)(2,1)S(1)}, u32[]{:S(2)}, u32[]{:S(2)}) collective-permute-start(bf16[128,2048]{1,0:T(8,128)(2,1)S(1)} %get-tuple-element.24), channel_id=1, source_target_pairs={{0,1},{1,0},{2,3},{3,2},{4,5},{5,4},{6,7},{7,6},{8,9},{9,8},{10,11... | collective-permute-start | bytes 1572872 | tf_op jit(solution)/shard_map/ppermute | solution.py:258
  65.5 9.2 %collective-permute-start.13 = (bf16[64,2048]{1,0:T(8,128)(2,1)S(1)}, bf16[64,2048]{1,0:T(8,128)(2,1)S(1)}, u32[]{:S(2)}, u32[]{:S(2)}) collective-permute-start(bf16[64,2048]{1,0:T(8,128)(2,1)S(1)} %get-tuple-element.33), channel_id=1, source_target_pairs={{0,2},{2,0},{4,6},{6,4},{8,10},{10,8},{12,14},{14,12},{1,3},{3,1},... | collective-permute-start | bytes 786440 | tf_op jit(solution)/shard_map/ppermute | solution.py:255
  68.7 24.5 %collective-permute-start.17 = (bf16[64,2048]{1,0:T(8,128)(2,1)S(1)}, bf16[64,2048]{1,0:T(8,128)(2,1)S(1)}, u32[]{:S(2)}, u32[]{:S(2)}) collective-permute-start(bf16[64,2048]{1,0:T(8,128)(2,1)S(1)} %get-tuple-element.37), channel_id=1, source_target_pairs={{0,2},{2,0},{4,6},{6,4},{8,10},{10,8},{12,14},{14,12},{1,3},{3,1},... | collective-permute-start | bytes 786440 | tf_op jit(solution)/shard_map/ppermute | solution.py:255
  70.0 15.9 %collective-permute-start.7 = (bf16[64,2048]{1,0:T(8,128)(2,1)S(1)}, bf16[64,2048]{1,0:T(8,128)(2,1)S(1)}, u32[]{:S(2)}, u32[]{:S(2)}) collective-permute-start(bf16[64,2048]{1,0:T(8,128)(2,1)S(1)} %get-tuple-element.27), channel_id=1, source_target_pairs={{0,2},{2,0},{4,6},{6,4},{8,10},{10,8},{12,14},{14,12},{1,3},{3,1},... | collective-permute-start | bytes 786440 | tf_op jit(solution)/shard_map/ppermute | solution.py:255
  74.8 18.4 %collective-permute-start.14 = (bf16[64,2048]{1,0:T(8,128)(2,1)S(1)}, bf16[64,2048]{1,0:T(8,128)(2,1)S(1)}, u32[]{:S(2)}, u32[]{:S(2)}) collective-permute-start(bf16[64,2048]{1,0:T(8,128)(2,1)S(1)} %add_convert_fusion.2), channel_id=1, source_target_pairs={{0,8},{2,10},{4,12},{6,14},{8,0},{10,2},{12,4},{14,6},{1,9},{3,11}... | collective-permute-start | bytes 786440 | tf_op jit(solution)/shard_map/ppermute | solution.py:255
  77.1 14.0 %collective-permute-start.15 = (bf16[64,2048]{1,0:T(8,128)(2,1)S(1)}, bf16[64,2048]{1,0:T(8,128)(2,1)S(1)}, u32[]{:S(2)}, u32[]{:S(2)}) collective-permute-start(bf16[64,2048]{1,0:T(8,128)(2,1)S(1)} %get-tuple-element.35), channel_id=1, source_target_pairs={{0,2},{2,0},{4,6},{6,4},{8,10},{10,8},{12,14},{14,12},{1,3},{3,1},... | collective-permute-start | bytes 786440 | tf_op jit(solution)/shard_map/ppermute | solution.py:255
  86.0 11.1 %collective-permute-start.8 = (bf16[64,2048]{1,0:T(8,128)(2,1)S(1)}, bf16[64,2048]{1,0:T(8,128)(2,1)S(1)}, u32[]{:S(2)}, u32[]{:S(2)}) collective-permute-start(bf16[64,2048]{1,0:T(8,128)(2,1)S(1)} %add_convert_fusion.3), channel_id=1, source_target_pairs={{0,12},{2,14},{4,8},{6,10},{8,4},{10,6},{12,0},{14,2},{1,13},{3,15... | collective-permute-start | bytes 786440 | tf_op jit(solution)/shard_map/ppermute | solution.py:255
  91.2 10.6 %collective-permute-start.16 = (bf16[64,2048]{1,0:T(8,128)(2,1)S(1)}, bf16[64,2048]{1,0:T(8,128)(2,1)S(1)}, u32[]{:S(2)}, u32[]{:S(2)}) collective-permute-start(bf16[64,2048]{1,0:T(8,128)(2,1)S(1)} %add_convert_fusion.1), channel_id=1, source_target_pairs={{0,4},{2,6},{4,0},{6,2},{8,12},{10,14},{12,8},{14,10},{1,5},{3,7},... | collective-permute-start | bytes 786440 | tf_op jit(solution)/shard_map/ppermute | solution.py:255

commit v3 on v2

--- a/solution.py
+++ b/solution.py
@@ -226,7 +226,11 @@
 
 
 def chunks_of(steps):
-    return [list(range(0, steps, 2)), list(range(1, steps, 2))]
+    return [[0], list(range(1, steps - 1)), [steps - 1]]
+
+
+def sent_as(step):
+    return {0: (F32, F32), 1: (BF16, BF16)}.get(step, (F32, BF16))
 
 
 def on_device(
@@ -279,7 +283,9 @@
     direct = [packet, cross(packet, 2)]
     for j in range(2, steps):
         direct.append(cross(direct[j - 1], 2) if j % 2 else cross(packet, 2 * j))
-    near = [cross(direct[j], 1) for j in range(steps)]
+    near = [cross(packet, 1)]
+    near.append(cross(near[0], 2))
+    near += [cross(direct[j], 1) for j in range(2, steps)]
 
     def load(*arrays):
         return call(
@@ -331,7 +337,7 @@
         tokens = (tok_rows, width)
         totals = call(
             functools.partial(mix_kernel, count, width, all_experts, capacity),
-            [shape(tokens, F32), shape(tokens, BF16)] * (count // 2),
+            [shape(tokens, t) for j in chunk for t in sent_as(j)],
             "v" * (count + 3),
             4 * count * tok_rows * capacity * width,
             8 * count * tok_rows * width,
@@ -340,12 +346,12 @@
         for i, j in enumerate(chunk):
             keeps[j], leaves[j] = totals[2 * i], totals[2 * i + 1]
 
-    mixed = None
-    for j in reversed(range(steps)):
+    other = leaves[0] + cross(leaves[1], 2).astype(F32)
+    mixed = keeps[0] + cross(keeps[1], 2).astype(F32)
+    for j in range(2, steps):
         both = keeps[j] + cross(leaves[j], 1).astype(F32)
-        term = both if j == 0 else cross(both.astype(BF16), 2 * j).astype(F32)
-        mixed = term if mixed is None else mixed + term
-    mixed = mixed.astype(BF16)
+        mixed = mixed + cross(both.astype(BF16), 2 * j).astype(F32)
+    mixed = (mixed + cross(other.astype(BF16), 1).astype(F32)).astype(BF16)
 
     penalty = call(
         functools.partial(

time: 104 us -> 99.9 us (0.961)
  waiting for transfers between devices: 50.1 us -> 41.8 us
  starting transfers between devices: 23.5 us -> 26 us
  Pallas kernels: 26.5 us -> 28.3 us
    ppermute x14, waiting for transfers between devices: 50.1 us -> 41.7 us  [cross(): lax.ppermute(block, 'expert', [(e, e ^ step) for e in range(expert_count)])]
    ppermute x14, starting transfers between devices: 22.7 us -> 24.5 us  [cross(): lax.ppermute(block, 'expert', [(e, e ^ step) for e in range(expert_count)])]
    pallas_call x12 -> x16, Pallas kernels: 26.5 us -> 28.3 us  [go(): return run(*args)]
  transfers between devices with their start and end apart: 18 -> 20, of which waited for: 11 -> 8; matrix products, arithmetic and copies ran while one was open for 0% -> 0% of each run, Pallas kernels for 24% -> 26%
where the time goes in v3:
time: 99.9 us; the launch traced here: 99.7 us
  waiting for transfers between devices  41.8 us (42%)
  Pallas kernels  28.3 us (28%)
  starting transfers between devices  26 us (26%)
  between operations  2.67 us (3%)
  other arithmetic  1 us (1%)
    ppermute x14, waiting for transfers between devices, cross(): lax.ppermute(block, 'expert', [(e, e ^ step) for e in range(expert_count)])  41.7 us
    pallas_call x16, Pallas kernels, go(): return run(*args)  28.3 us
    ppermute x14, starting transfers between devices, cross(): lax.ppermute(block, 'expert', [(e, e ^ step) for e in range(expert_count)])  24.5 us
  transfers between devices with their start and end apart: 20, of which 8 were waited for; matrix products, arithmetic and copies ran while one was open for 0% of the time, Pallas kernels for 26%

profile of v3, /device:TPU:0, one launch (start us, length us, event | category | flops | bytes accessed | tf_op | source)
XLA Modules:
  0.0 99.7 jit_solution(14052486527895825185)
XLA Ops:
  1.3 1.6 %shard_map.95.refs_0_ = bf16[64,2176]{1,0:T(8,128)(2,1)S(1)} custom-call(s32[1]{0:T(128)S(6)} %copy.11.live_ref, bf16[64,2048]{1,0:T(8,128)(2,1)} %hidden_hbm.1, f32[1,2048]{1,0:T(1,128)} %bitcast.12, bf16[16,2048]{1,0:T(8,128)(2,1)} %bitcast.11, s32[6,64]{1,0:T(8,128)} %bitcast.13), custom_call_target="tpu_custom_call" | custom-call | flops 4194304 | bytes 524288 | tf_op jit(solution)/shard_map/pallas_call | solution.py:223
  2.9 4.1 %collective-permute-start.5 = (bf16[64,2176]{1,0:T(8,128)(2,1)S(1)}, bf16[64,2176]{1,0:T(8,128)(2,1)S(1)}, u32[]{:S(2)}, u32[]{:S(2)}) collective-permute-start(bf16[64,2176]{1,0:T(8,128)(2,1)S(1)} %shard_map.95.refs_0_), channel_id=1, source_target_pairs={{0,8},{2,10},{4,12},{6,14},{8,0},{10,2},{12,4},{14,6},{1,9},{3,11}... | collective-permute-start | bytes 835592 | tf_op jit(solution)/shard_map/ppermute | solution.py:259
  7.0 1.5 %collective-permute-start = (bf16[64,2176]{1,0:T(8,128)(2,1)S(1)}, bf16[64,2176]{1,0:T(8,128)(2,1)S(1)}, u32[]{:S(2)}, u32[]{:S(2)}) collective-permute-start(bf16[64,2176]{1,0:T(8,128)(2,1)S(1)} %shard_map.95.refs_0_), channel_id=1, source_target_pairs={{0,2},{2,0},{4,6},{6,4},{8,10},{10,8},{12,14},{14,12},{1,3},{3,1},... | collective-permute-start | bytes 835592 | tf_op jit(solution)/shard_map/ppermute | solution.py:259
  8.6 1.6 %collective-permute-start.3 = (bf16[64,2176]{1,0:T(8,128)(2,1)S(1)}, bf16[64,2176]{1,0:T(8,128)(2,1)S(1)}, u32[]{:S(2)}, u32[]{:S(2)}) collective-permute-start(bf16[64,2176]{1,0:T(8,128)(2,1)S(1)} %shard_map.95.refs_0_), channel_id=1, source_target_pairs={{0,4},{2,6},{4,0},{6,2},{8,12},{10,14},{12,8},{14,10},{1,5},{3,7},... | collective-permute-start | bytes 835592 | tf_op jit(solution)/shard_map/ppermute | solution.py:259
  10.1 9.6 %collective-permute-done.5.refs_2_ = bf16[64,2176]{1,0:T(8,128)(2,1)S(1)} collective-permute-done((bf16[64,2176]{1,0:T(8,128)(2,1)S(1)}, bf16[64,2176]{1,0:T(8,128)(2,1)S(1)}, u32[]{:S(2)}, u32[]{:S(2)}) %collective-permute-start.5) | collective-permute-done | bytes 278560 | tf_op jit(solution)/shard_map/ppermute | solution.py:259
  19.8 1.6 %collective-permute-start.6 = (bf16[64,2176]{1,0:T(8,128)(2,1)S(1)}, bf16[64,2176]{1,0:T(8,128)(2,1)S(1)}, u32[]{:S(2)}, u32[]{:S(2)}) collective-permute-start(bf16[64,2176]{1,0:T(8,128)(2,1)S(1)} %collective-permute-done.5.refs_2_), channel_id=1, source_target_pairs={{0,2},{2,0},{4,6},{6,4},{8,10},{10,8},{12,14},{14,12},{1,3},{3,1},... | collective-permute-start | bytes 835592 | tf_op jit(solution)/shard_map/ppermute | solution.py:259
  21.9 5.6 %collective-permute-done.6.refs_3_ = bf16[64,2176]{1,0:T(8,128)(2,1)S(1)} collective-permute-done((bf16[64,2176]{1,0:T(8,128)(2,1)S(1)}, bf16[64,2176]{1,0:T(8,128)(2,1)S(1)}, u32[]{:S(2)}, u32[]{:S(2)}) %collective-permute-start.6) | collective-permute-done | bytes 278560 | tf_op jit(solution)/shard_map/ppermute | solution.py:259
  29.3 1.7 %collective-permute-start.12 = (bf16[64,2176]{1,0:T(8,128)(2,1)S(1)}, bf16[64,2176]{1,0:T(8,128)(2,1)S(1)}, u32[]{:S(2)}, u32[]{:S(2)}) collective-permute-start(bf16[64,2176]{1,0:T(8,128)(2,1)S(1)} %collective-permute-done.5.refs_2_), channel_id=1, source_target_pairs={{0,4},{2,6},{4,0},{6,2},{8,12},{10,14},{12,8},{14,10},{1,5},{3,7},... | collective-permute-start | bytes 835592 | tf_op jit(solution)/shard_map/ppermute | solution.py:259
  31.0 7.3 %collective-permute-done.12.refs_0_ = bf16[64,2176]{1,0:T(8,128)(2,1)S(1)} collective-permute-done((bf16[64,2176]{1,0:T(8,128)(2,1)S(1)}, bf16[64,2176]{1,0:T(8,128)(2,1)S(1)}, u32[]{:S(2)}, u32[]{:S(2)}) %collective-permute-start.12) | collective-permute-done | bytes 278560 | tf_op jit(solution)/shard_map/ppermute | solution.py:259
  39.1 4.3 %shard_map.97.up_ref = bf16[2048,2816]{1,0:T(8,128)(2,1)S(1)} custom-call(bf16[2048,2816]{1,0:T(8,128)(2,1)} %bitcast.8), custom_call_target="tpu_custom_call" | custom-call | bytes 11534336 | tf_op jit(solution)/shard_map/pallas_call | solution.py:223
  43.4 3.9 %shard_map.98 = (bf16[1408,2048]{1,0:T(8,128)(2,1)S(1)}, bf16[3,352,2048]{2,1,0:T(8,128)(2,1)S(1)}) custom-call(bf16[1408,2048]{1,0:T(8,128)(2,1)} %bitcast.9, bf16[3,352,2048]{2,1,0:T(8,128)(2,1)} %bitcast.10), custom_call_target="tpu_custom_call" | custom-call | bytes 10092544 | tf_op jit(solution)/shard_map/pallas_call | solution.py:223
  48.9 5.0 %shard_map.103 = (bf16[128,2048]{1,0:T(8,128)(2,1)S(1)}, bf16[128,2048]{1,0:T(8,128)(2,1)S(1)}) custom-call(bf16[144,2048]{1,0:T(8,128)(2,1)S(1)} %get-tuple-element.31.mine_ref, bf16[144,2048]{1,0:T(8,128)(2,1)S(1)} %collective-permute-done.7.peer_ref, bf16[2048,2816]{1,0:T(8,128)(2,1)S(1)} %shard_map.97.up_ref, ...), custom_call_target="tpu_custom_call" | custom-call | flops 4429185024 | bytes 17301504 | tf_op jit(solution)/shard_map/pallas_call | solution.py:223
  54.1 2.6 %shard_map.107 = (bf16[64,2048]{1,0:T(8,128)(2,1)S(1)}, bf16[64,2048]{1,0:T(8,128)(2,1)S(1)}) custom-call(bf16[80,2048]{1,0:T(8,128)(2,1)S(1)} %get-tuple-element.38.mine_ref, bf16[80,2048]{1,0:T(8,128)(2,1)S(1)} %collective-permute-done.14.peer_ref, bf16[2048,2816]{1,0:T(8,128)(2,1)S(1)} %shard_map.97.up_ref, bf16[1408,2048]{1,0:T(8,128)(2,1)S(1)} %get-tuple-element.26.down_ref), custom_call_target="tpu_custom_call" | custom-call | flops 2214592512 | bytes 17301504 | tf_op jit(solution)/shard_map/pallas_call | solution.py:223
  57.3 2.6 %shard_map.99 = (bf16[64,2048]{1,0:T(8,128)(2,1)S(1)}, bf16[64,2048]{1,0:T(8,128)(2,1)S(1)}) custom-call(bf16[80,2048]{1,0:T(8,128)(2,1)S(1)} %get-tuple-element.24.mine_ref, bf16[80,2048]{1,0:T(8,128)(2,1)S(1)} %collective-permute-done.1.peer_ref, bf16[2048,2816]{1,0:T(8,128)(2,1)S(1)} %shard_map.97.up_ref, bf16[1408,2048]{1,0:T(8,128)(2,1)S(1)} %get-tuple-element.26.down_ref), custom_call_target="tpu_custom_call" | custom-call | flops 2214592512 | bytes 17301504 | tf_op jit(solution)/shard_map/pallas_call | solution.py:223
  60.0 1.4 %shard_map.108.refs_4_ = f32[128,2048]{1,0:T(8,128)S(1)} custom-call(bf16[64,2176]{1,0:T(8,128)(2,1)S(1)} %collective-permute-done.12.refs_0_, bf16[64,2176]{1,0:T(8,128)(2,1)S(1)} %collective-permute-done.13.refs_1_, bf16[3,352,2048]{2,1,0:T(8,128)(2,1)S(1)} %get-tuple-element.29.refs_2_.refs_4_), custom_call_target="tpu_custom_call" | custom-call | flops 553648128 | bytes 4325376 | tf_op jit(solution)/shard_map/pallas_call | solution.py:223
  61.8 1.4 %collective-permute-start.16 = (bf16[64,2048]{1,0:T(8,128)(2,1)S(1)}, bf16[64,2048]{1,0:T(8,128)(2,1)S(1)}, u32[]{:S(2)}, u32[]{:S(2)}) collective-permute-start(bf16[64,2048]{1,0:T(8,128)(2,1)S(1)} %get-tuple-element.43), channel_id=1, source_target_pairs={{0,2},{2,0},{4,6},{6,4},{8,10},{10,8},{12,14},{14,12},{1,3},{3,1},... | collective-permute-start | bytes 786440 | tf_op jit(solution)/shard_map/ppermute | solution.py:259
  63.2 1.6 %shard_map.100.refs_4_ = f32[128,2048]{1,0:T(8,128)S(1)} custom-call(bf16[64,2176]{1,0:T(8,128)(2,1)S(1)} %shard_map.95.refs_0_, bf16[64,2176]{1,0:T(8,128)(2,1)S(1)} %collective-permute-done.refs_1_, bf16[3,352,2048]{2,1,0:T(8,128)(2,1)S(1)} %get-tuple-element.29.refs_2_.refs_4_), custom_call_target="tpu_custom_call" | custom-call | flops 553648128 | bytes 4325376 | tf_op jit(solution)/shard_map/pallas_call | solution.py:223
  64.8 1.9 %shard_map.104.refs_6_ = f32[256,2048]{1,0:T(8,128)S(1)} custom-call(bf16[64,2176]{1,0:T(8,128)(2,1)S(1)} %collective-permute-done.3.refs_0_, bf16[64,2176]{1,0:T(8,128)(2,1)S(1)} %collective-permute-done.4.refs_1_, bf16[64,2176]{1,0:T(8,128)(2,1)S(1)} %collective-permute-done.5.refs_2_, bf16[64,2176]{1,0:T(8,128)(2,1)S(1)} %collective-permute-done.6.refs_3_, ...), custom_call_target="tpu_custom_call" | custom-call | flops 1107296256 | bytes 4325376 | tf_op jit(solution)/shard_map/pallas_call | solution.py:223
  67.6 1.7 %collective-permute-start.9 = (bf16[64,2048]{1,0:T(8,128)(2,1)S(1)}, bf16[64,2048]{1,0:T(8,128)(2,1)S(1)}, u32[]{:S(2)}, u32[]{:S(2)}) collective-permute-start(bf16[64,2048]{1,0:T(8,128)(2,1)S(1)} %get-tuple-element.35), channel_id=1, source_target_pairs={{0,4},{2,6},{4,0},{6,2},{8,12},{10,14},{12,8},{14,10},{1,5},{3,7},... | collective-permute-start | bytes 786440 | tf_op jit(solution)/shard_map/ppermute | solution.py:259
  70.6 4.4 %collective-permute-start.17 = (bf16[64,2048]{1,0:T(8,128)(2,1)S(1)}, bf16[64,2048]{1,0:T(8,128)(2,1)S(1)}, u32[]{:S(2)}, u32[]{:S(2)}) collective-permute-start(bf16[64,2048]{1,0:T(8,128)(2,1)S(1)} %add_convert_fusion.2), channel_id=1, source_target_pairs={{0,12},{2,14},{4,8},{6,10},{8,4},{10,6},{12,0},{14,2},{1,13},{3,15... | collective-permute-start | bytes 786440 | tf_op jit(solution)/shard_map/ppermute | solution.py:259
  75.0 2.4 %collective-permute-done.10 = bf16[64,2048]{1,0:T(8,128)(2,1)S(1)} collective-permute-done((bf16[64,2048]{1,0:T(8,128)(2,1)S(1)}, bf16[64,2048]{1,0:T(8,128)(2,1)S(1)}, u32[]{:S(2)}, u32[]{:S(2)}) %collective-permute-start.10) | collective-permute-done | bytes 262176 | tf_op jit(solution)/shard_map/ppermute | solution.py:259
  77.5 3.4 %collective-permute-start.11 = (bf16[64,2048]{1,0:T(8,128)(2,1)S(1)}, bf16[64,2048]{1,0:T(8,128)(2,1)S(1)}, u32[]{:S(2)}, u32[]{:S(2)}) collective-permute-start(bf16[64,2048]{1,0:T(8,128)(2,1)S(1)} %add_convert_fusion.3), channel_id=1, source_target_pairs={{0,8},{2,10},{4,12},{6,14},{8,0},{10,2},{12,4},{14,6},{1,9},{3,11}... | collective-permute-start | bytes 786440 | tf_op jit(solution)/shard_map/ppermute | solution.py:259
  80.9 10.0 %collective-permute-done.18 = bf16[64,2048]{1,0:T(8,128)(2,1)S(1)} collective-permute-done((bf16[64,2048]{1,0:T(8,128)(2,1)S(1)}, bf16[64,2048]{1,0:T(8,128)(2,1)S(1)}, u32[]{:S(2)}, u32[]{:S(2)}) %collective-permute-start.18) | collective-permute-done | bytes 262176 | tf_op jit(solution)/shard_map/ppermute | solution.py:259
  92.3 5.5 %collective-permute-done.11 = bf16[64,2048]{1,0:T(8,128)(2,1)S(1)} collective-permute-done((bf16[64,2048]{1,0:T(8,128)(2,1)S(1)}, bf16[64,2048]{1,0:T(8,128)(2,1)S(1)}, u32[]{:S(2)}, u32[]{:S(2)}) %collective-permute-start.11) | collective-permute-done | bytes 262176 | tf_op jit(solution)/shard_map/ppermute | solution.py:259
  (42 shorter events, 10.1 us)
Async XLA Ops:
  2.9 16.9 %collective-permute-start.5 = (bf16[64,2176]{1,0:T(8,128)(2,1)S(1)}, bf16[64,2176]{1,0:T(8,128)(2,1)S(1)}, u32[]{:S(2)}, u32[]{:S(2)}) collective-permute-start(bf16[64,2176]{1,0:T(8,128)(2,1)S(1)} %shard_map.95.refs_0_), channel_id=1, source_target_pairs={{0,8},{2,10},{4,12},{6,14},{8,0},{10,2},{12,4},{14,6},{1,9},{3,11}... | collective-permute-start | bytes 835592 | tf_op jit(solution)/shard_map/ppermute | solution.py:259
  7.0 14.3 %collective-permute-start = (bf16[64,2176]{1,0:T(8,128)(2,1)S(1)}, bf16[64,2176]{1,0:T(8,128)(2,1)S(1)}, u32[]{:S(2)}, u32[]{:S(2)}) collective-permute-start(bf16[64,2176]{1,0:T(8,128)(2,1)S(1)} %shard_map.95.refs_0_), channel_id=1, source_target_pairs={{0,2},{2,0},{4,6},{6,4},{8,10},{10,8},{12,14},{14,12},{1,3},{3,1},... | collective-permute-start | bytes 835592 | tf_op jit(solution)/shard_map/ppermute | solution.py:259
  8.6 13.4 %collective-permute-start.3 = (bf16[64,2176]{1,0:T(8,128)(2,1)S(1)}, bf16[64,2176]{1,0:T(8,128)(2,1)S(1)}, u32[]{:S(2)}, u32[]{:S(2)}) collective-permute-start(bf16[64,2176]{1,0:T(8,128)(2,1)S(1)} %shard_map.95.refs_0_), channel_id=1, source_target_pairs={{0,4},{2,6},{4,0},{6,2},{8,12},{10,14},{12,8},{14,10},{1,5},{3,7},... | collective-permute-start | bytes 835592 | tf_op jit(solution)/shard_map/ppermute | solution.py:259
  19.8 7.8 %collective-permute-start.6 = (bf16[64,2176]{1,0:T(8,128)(2,1)S(1)}, bf16[64,2176]{1,0:T(8,128)(2,1)S(1)}, u32[]{:S(2)}, u32[]{:S(2)}) collective-permute-start(bf16[64,2176]{1,0:T(8,128)(2,1)S(1)} %collective-permute-done.5.refs_2_), channel_id=1, source_target_pairs={{0,2},{2,0},{4,6},{6,4},{8,10},{10,8},{12,14},{14,12},{1,3},{3,1},... | collective-permute-start | bytes 835592 | tf_op jit(solution)/shard_map/ppermute | solution.py:259
  21.3 7.2 %collective-permute-start.4 = (bf16[64,2176]{1,0:T(8,128)(2,1)S(1)}, bf16[64,2176]{1,0:T(8,128)(2,1)S(1)}, u32[]{:S(2)}, u32[]{:S(2)}) collective-permute-start(bf16[64,2176]{1,0:T(8,128)(2,1)S(1)} %collective-permute-done.refs_1_), channel_id=1, source_target_pairs={{0,4},{2,6},{4,0},{6,2},{8,12},{10,14},{12,8},{14,10},{1,5},{3,7},... | collective-permute-start | bytes 835592 | tf_op jit(solution)/shard_map/ppermute | solution.py:259
  29.3 19.7 %collective-permute-start.7 = (bf16[144,2048]{1,0:T(8,128)(2,1)S(1)}, bf16[144,2048]{1,0:T(8,128)(2,1)S(1)}, u32[]{:S(2)}, u32[]{:S(2)}) collective-permute-start(bf16[144,2048]{1,0:T(8,128)(2,1)S(1)} %get-tuple-element.32), channel_id=1, source_target_pairs={{0,1},{1,0},{2,3},{3,2},{4,5},{5,4},{6,7},{7,6},{8,9},{9,8},{10,11... | collective-permute-start | bytes 1769480 | tf_op jit(solution)/shard_map/ppermute | solution.py:262
  29.3 9.1 %collective-permute-start.12 = (bf16[64,2176]{1,0:T(8,128)(2,1)S(1)}, bf16[64,2176]{1,0:T(8,128)(2,1)S(1)}, u32[]{:S(2)}, u32[]{:S(2)}) collective-permute-start(bf16[64,2176]{1,0:T(8,128)(2,1)S(1)} %collective-permute-done.5.refs_2_), channel_id=1, source_target_pairs={{0,4},{2,6},{4,0},{6,2},{8,12},{10,14},{12,8},{14,10},{1,5},{3,7},... | collective-permute-start | bytes 835592 | tf_op jit(solution)/shard_map/ppermute | solution.py:259
  38.4 9.5 %collective-permute-start.13 = (bf16[64,2176]{1,0:T(8,128)(2,1)S(1)}, bf16[64,2176]{1,0:T(8,128)(2,1)S(1)}, u32[]{:S(2)}, u32[]{:S(2)}) collective-permute-start(bf16[64,2176]{1,0:T(8,128)(2,1)S(1)} %collective-permute-done.12.refs_0_), channel_id=1, source_target_pairs={{0,2},{2,0},{4,6},{6,4},{8,10},{10,8},{12,14},{14,12},{1,3},{3,1},... | collective-permute-start | bytes 835592 | tf_op jit(solution)/shard_map/ppermute | solution.py:259
  47.8 9.5 %collective-permute-start.1 = (bf16[80,2048]{1,0:T(8,128)(2,1)S(1)}, bf16[80,2048]{1,0:T(8,128)(2,1)S(1)}, u32[]{:S(2)}, u32[]{:S(2)}) collective-permute-start(bf16[80,2048]{1,0:T(8,128)(2,1)S(1)} %get-tuple-element.25), channel_id=1, source_target_pairs={{0,1},{1,0},{2,3},{3,2},{4,5},{5,4},{6,7},{7,6},{8,9},{9,8},{10,11... | collective-permute-start | bytes 983048 | tf_op jit(solution)/shard_map/ppermute | solution.py:262
  48.4 5.7 %collective-permute-start.14 = (bf16[80,2048]{1,0:T(8,128)(2,1)S(1)}, bf16[80,2048]{1,0:T(8,128)(2,1)S(1)}, u32[]{:S(2)}, u32[]{:S(2)}) collective-permute-start(bf16[80,2048]{1,0:T(8,128)(2,1)S(1)} %get-tuple-element.39), channel_id=1, source_target_pairs={{0,1},{1,0},{2,3},{3,2},{4,5},{5,4},{6,7},{7,6},{8,9},{9,8},{10,11... | collective-permute-start | bytes 983048 | tf_op jit(solution)/shard_map/ppermute | solution.py:262
  54.0 13.1 %collective-permute-start.8 = (bf16[128,2048]{1,0:T(8,128)(2,1)S(1)}, bf16[128,2048]{1,0:T(8,128)(2,1)S(1)}, u32[]{:S(2)}, u32[]{:S(2)}) collective-permute-start(bf16[128,2048]{1,0:T(8,128)(2,1)S(1)} %get-tuple-element.34), channel_id=1, source_target_pairs={{0,1},{1,0},{2,3},{3,2},{4,5},{5,4},{6,7},{7,6},{8,9},{9,8},{10,11... | collective-permute-start | bytes 1572872 | tf_op jit(solution)/shard_map/ppermute | solution.py:262
  56.7 4.7 %collective-permute-start.15 = (bf16[64,2048]{1,0:T(8,128)(2,1)S(1)}, bf16[64,2048]{1,0:T(8,128)(2,1)S(1)}, u32[]{:S(2)}, u32[]{:S(2)}) collective-permute-start(bf16[64,2048]{1,0:T(8,128)(2,1)S(1)} %get-tuple-element.41), channel_id=1, source_target_pairs={{0,1},{1,0},{2,3},{3,2},{4,5},{5,4},{6,7},{7,6},{8,9},{9,8},{10,11... | collective-permute-start | bytes 786440 | tf_op jit(solution)/shard_map/ppermute | solution.py:262
  59.9 6.7 %collective-permute-start.2 = (bf16[64,2048]{1,0:T(8,128)(2,1)S(1)}, bf16[64,2048]{1,0:T(8,128)(2,1)S(1)}, u32[]{:S(2)}, u32[]{:S(2)}) collective-permute-start(bf16[64,2048]{1,0:T(8,128)(2,1)S(1)} %get-tuple-element.28), channel_id=1, source_target_pairs={{0,1},{1,0},{2,3},{3,2},{4,5},{5,4},{6,7},{7,6},{8,9},{9,8},{10,11... | collective-permute-start | bytes 786440 | tf_op jit(solution)/shard_map/ppermute | solution.py:262
  61.8 8.8 %collective-permute-start.16 = (bf16[64,2048]{1,0:T(8,128)(2,1)S(1)}, bf16[64,2048]{1,0:T(8,128)(2,1)S(1)}, u32[]{:S(2)}, u32[]{:S(2)}) collective-permute-start(bf16[64,2048]{1,0:T(8,128)(2,1)S(1)} %get-tuple-element.43), channel_id=1, source_target_pairs={{0,2},{2,0},{4,6},{6,4},{8,10},{10,8},{12,14},{14,12},{1,3},{3,1},... | collective-permute-start | bytes 786440 | tf_op jit(solution)/shard_map/ppermute | solution.py:259
  67.6 24.7 %collective-permute-start.9 = (bf16[64,2048]{1,0:T(8,128)(2,1)S(1)}, bf16[64,2048]{1,0:T(8,128)(2,1)S(1)}, u32[]{:S(2)}, u32[]{:S(2)}) collective-permute-start(bf16[64,2048]{1,0:T(8,128)(2,1)S(1)} %get-tuple-element.35), channel_id=1, source_target_pairs={{0,4},{2,6},{4,0},{6,2},{8,12},{10,14},{12,8},{14,10},{1,5},{3,7},... | collective-permute-start | bytes 786440 | tf_op jit(solution)/shard_map/ppermute | solution.py:259
  69.3 8.1 %collective-permute-start.10 = (bf16[64,2048]{1,0:T(8,128)(2,1)S(1)}, bf16[64,2048]{1,0:T(8,128)(2,1)S(1)}, u32[]{:S(2)}, u32[]{:S(2)}) collective-permute-start(bf16[64,2048]{1,0:T(8,128)(2,1)S(1)} %get-tuple-element.37), channel_id=1, source_target_pairs={{0,2},{2,0},{4,6},{6,4},{8,10},{10,8},{12,14},{14,12},{1,3},{3,1},... | collective-permute-start | bytes 786440 | tf_op jit(solution)/shard_map/ppermute | solution.py:259
  69.8 21.1 %collective-permute-start.18 = (bf16[64,2048]{1,0:T(8,128)(2,1)S(1)}, bf16[64,2048]{1,0:T(8,128)(2,1)S(1)}, u32[]{:S(2)}, u32[]{:S(2)}) collective-permute-start(bf16[64,2048]{1,0:T(8,128)(2,1)S(1)} %get-tuple-element.45), channel_id=1, source_target_pairs={{0,4},{2,6},{4,0},{6,2},{8,12},{10,14},{12,8},{14,10},{1,5},{3,7},... | collective-permute-start | bytes 786440 | tf_op jit(solution)/shard_map/ppermute | solution.py:259
  70.6 21.6 %collective-permute-start.17 = (bf16[64,2048]{1,0:T(8,128)(2,1)S(1)}, bf16[64,2048]{1,0:T(8,128)(2,1)S(1)}, u32[]{:S(2)}, u32[]{:S(2)}) collective-permute-start(bf16[64,2048]{1,0:T(8,128)(2,1)S(1)} %add_convert_fusion.2), channel_id=1, source_target_pairs={{0,12},{2,14},{4,8},{6,10},{8,4},{10,6},{12,0},{14,2},{1,13},{3,15... | collective-permute-start | bytes 786440 | tf_op jit(solution)/shard_map/ppermute | solution.py:259
  77.5 20.2 %collective-permute-start.11 = (bf16[64,2048]{1,0:T(8,128)(2,1)S(1)}, bf16[64,2048]{1,0:T(8,128)(2,1)S(1)}, u32[]{:S(2)}, u32[]{:S(2)}) collective-permute-start(bf16[64,2048]{1,0:T(8,128)(2,1)S(1)} %add_convert_fusion.3), channel_id=1, source_target_pairs={{0,8},{2,10},{4,12},{6,14},{8,0},{10,2},{12,4},{14,6},{1,9},{3,11}... | collective-permute-start | bytes 786440 | tf_op jit(solution)/shard_map/ppermute | solution.py:259
  91.0 6.7 %collective-permute-start.19 = (bf16[64,2048]{1,0:T(8,128)(2,1)S(1)}, bf16[64,2048]{1,0:T(8,128)(2,1)S(1)}, u32[]{:S(2)}, u32[]{:S(2)}) collective-permute-start(bf16[64,2048]{1,0:T(8,128)(2,1)S(1)} %add_convert_fusion.1), channel_id=1, source_target_pairs={{0,2},{2,0},{4,6},{6,4},{8,10},{10,8},{12,14},{14,12},{1,3},{3,1},... | collective-permute-start | bytes 786440 | tf_op jit(solution)/shard_map/ppermute | solution.py:259

commit v4 on v3

--- a/solution.py
+++ b/solution.py
@@ -149,17 +149,25 @@
 
 
 def shared_kernel(count, width, *refs):
-    blocks, (weights_ref, out_ref) = refs[:count], refs[count:]
+    blocks, weights_ref, outs = refs[:count], refs[count], refs[count + 1 :]
     states = jnp.concatenate([b[:, :width] for b in blocks], axis=0)
     across = (((1,), (1,)), ((), ()))
     gate = lax.dot_general(states, weights_ref[0], across, preferred_element_type=F32)
     up = lax.dot_general(states, weights_ref[1], across, preferred_element_type=F32)
     active = (silu(gate) * up).astype(BF16)
-    out_ref[...] = jnp.dot(active, weights_ref[2], preferred_element_type=F32)
-
-
-def mix_kernel(count, width, experts, capacity, *refs):
-    blocks, (mine_ref, peer_ref, shared_ref), outs = refs[:count], refs[count : count + 3], refs[count + 3 :]
+    at = 0
+    for out in outs:
+        rows = active[at : at + out.shape[0]]
+        out[...] = jnp.dot(rows, weights_ref[2], preferred_element_type=F32)
+        at += out.shape[0]
+
+
+def mix_kernel(count, width, experts, capacity, cuts, *refs):
+    blocks, (mine_ref, peer_ref, shared_ref) = refs[:count], refs[count : count + 3]
+    outs, at = [], count + 3
+    for pieces in cuts:
+        outs.append(refs[at : at + pieces])
+        at += pieces
     me, peer = my_seat()
     rows = blocks[0].shape[0]
     for i, block in enumerate(blocks):
@@ -171,7 +179,29 @@
         total = shared_ref[i * rows : (i + 1) * rows, :] + jnp.dot(
             mixing, results, preferred_element_type=F32
         )
-        outs[i][...] = total.astype(outs[i].dtype)
+        at = 0
+        for out in outs[i]:
+            out[...] = total[:, at : at + out.shape[1]].astype(out.dtype)
+            at += out.shape[1]
+
+
+def add_kernel(keep_ref, more_ref, out_ref):
+    out_ref[...] = (keep_ref[...] + more_ref[...].astype(F32)).astype(out_ref.dtype)
+
+
+def sum_kernel(*refs):
+    pieces, out_ref = refs[:-1], refs[-1]
+    total, at, width = None, 0, out_ref.shape[1]
+    sums = []
+    for piece in pieces:
+        sums.append((at, piece[...].astype(F32)))
+        at = (at + piece.shape[1]) % width
+    whole = [x for _, x in sums if x.shape[1] == width]
+    total = functools.reduce(lambda x, y: x + y, whole)
+    for at, x in sums:
+        if x.shape[1] < width:
+            to = at + x.shape[1]
+            out_ref[:, at:to] = (total[:, at:to] + x).astype(out_ref.dtype)
 
 
 def penalty_kernel(experts, scale, steps, *refs):
@@ -197,13 +227,13 @@
     out_ref[...] = jnp.sum(load * mass, axis=1, keepdims=True) * experts / scale
 
 
-def call(kernel, out_shape, where, flops, nbytes, mib, scratch=()):
+def call(kernel, out_shape, where, flops, nbytes, mib, scratch=(), out="v"):
     spaces = {"v": pltpu.VMEM, "s": pltpu.SMEM, "h": pltpu.HBM}
     many = isinstance(out_shape, (list, tuple))
     specs = {"v": VMEM, "s": SMEM, "h": pl.BlockSpec(memory_space=pltpu.HBM)}
 
     def vmem(x):
-        return pltpu.VMEM(x.shape, x.dtype)
+        return pltpu.VMEM(x.shape, x.dtype) if out == "v" else x
 
     run = pl.pallas_call(
         kernel,
@@ -226,11 +256,15 @@
 
 
 def chunks_of(steps):
-    return [[0], list(range(1, steps - 1)), [steps - 1]]
+    return [[0], list(range(2, steps, 2)), list(range(1, steps, 2))]
 
 
 def sent_as(step):
     return {0: (F32, F32), 1: (BF16, BF16)}.get(step, (F32, BF16))
+
+
+def pieces_of(step, steps):
+    return 2 if step == steps - 1 else 1
 
 
 def on_device(
@@ -300,9 +334,23 @@
 
     (gate_up,) = load(routed_gate_up[0])
     down, shared_rows = load(routed_down[0], jnp.swapaxes(shared_weights, 1, 2))
+    arrived = [(direct[j], near[j]) for j in range(steps)]
+
+    def shared_sums(chunks):
+        blocks = [b for chunk in chunks for j in chunk for b in arrived[j]]
+        return call(
+            functools.partial(shared_kernel, len(blocks), width),
+            [shape((2 * len(chunk) * tok_rows, width), F32) for chunk in chunks],
+            "v" * (len(blocks) + 1),
+            6 * len(blocks) * tok_rows * width * shared_rows.shape[1],
+            6 * width * shared_rows.shape[1],
+            8,
+        )(*blocks, shared_rows)
+
+    shared = shared_sums(chunks[:2]) + shared_sums(chunks[2:])
     keeps, leaves, sums = [None] * steps, [None] * steps, []
-    for chunk in chunks:
-        blocks = [b for j in chunk for b in (direct[j], near[j])]
+    for c, chunk in enumerate(chunks):
+        blocks = [b for j in chunk for b in arrived[j]]
         count = len(blocks)
         picked = shape((count * capacity + 16, width), BF16)
         results = shape((count * capacity, width), BF16)
@@ -315,14 +363,6 @@
             8,
         )(*blocks)
         theirs = swap(theirs)
-        shared = call(
-            functools.partial(shared_kernel, count, width),
-            shape((count * tok_rows, width), F32),
-            "v" * (count + 1),
-            6 * count * tok_rows * width * shared_rows.shape[1],
-            6 * width * shared_rows.shape[1],
-            8,
-        )(*blocks, shared_rows)
         sums += [x[count * capacity :][:count, :lanes] for x in (mine, theirs)]
         mine, theirs = call(
             expert_kernel,
@@ -334,24 +374,31 @@
             [pltpu.VMEM((2 * count * capacity, hidden_units), BF16)],
         )(mine, theirs, gate_up, down)
         theirs = swap(theirs)
-        tokens = (tok_rows, width)
+        cuts = [pieces_of(j, steps) for j in chunk for _ in range(2)]
+        kinds = [t for j in chunk for t in sent_as(j)]
         totals = call(
-            functools.partial(mix_kernel, count, width, all_experts, capacity),
-            [shape(tokens, t) for j in chunk for t in sent_as(j)],
+            functools.partial(mix_kernel, count, width, all_experts, capacity, cuts),
+            [shape((tok_rows, width // n), t) for n, t in zip(cuts, kinds) for _ in range(n)],
             "v" * (count + 3),
             4 * count * tok_rows * capacity * width,
             8 * count * tok_rows * width,
             8,
-        )(*blocks, mine, theirs, shared)
-        for i, j in enumerate(chunk):
-            keeps[j], leaves[j] = totals[2 * i], totals[2 * i + 1]
-
-    other = leaves[0] + cross(leaves[1], 2).astype(F32)
-    mixed = keeps[0] + cross(keeps[1], 2).astype(F32)
+        )(*blocks, mine, theirs, shared[c])
+        for j in chunk:
+            pieces = pieces_of(j, steps)
+            keeps[j], leaves[j], totals = totals[:pieces], totals[pieces : 2 * pieces], totals[2 * pieces :]
+
+    def add(keep, more):
+        return call(add_kernel, shape(keep.shape, BF16), "vv", 0, 0, 4)(keep, more)
+
+    other = add(leaves[0][0], cross(leaves[1][0], 2))
+    terms = [keeps[0][0], cross(keeps[1][0], 2)]
     for j in range(2, steps):
-        both = keeps[j] + cross(leaves[j], 1).astype(F32)
-        mixed = mixed + cross(both.astype(BF16), 2 * j).astype(F32)
-    mixed = (mixed + cross(other.astype(BF16), 1).astype(F32)).astype(BF16)
+        for keep, leave in zip(keeps[j], leaves[j]):
+            both = add(keep, cross(leave, 1))
+            terms.append(cross(both, 2 * j))
+    terms.append(cross(other, 1))
+    mixed = call(sum_kernel, shape((tok_rows, width), BF16), "v" * len(terms), 0, 0, 8, out="h")(*terms)
 
     penalty = call(
         functools.partial(

time: 99.9 us -> 103 us (1.031)
  the two profiles are of different devices: /device:TPU:0 before, /device:TPU:19 now
where the time goes in v4:
time: 103 us
  waiting for transfers between devices  47.8 us (46%)
  Pallas kernels  28.4 us (28%)
  starting transfers between devices  23.8 us (23%)
  between operations  2.63 us (3%)
    ppermute x16, waiting for transfers between devices, cross(): lax.ppermute(block, 'expert', [(e, e ^ step) for e in range(expert_count)])  47.8 us
    pallas_call x20, Pallas kernels, go(): return run(*args)  28.4 us
    ppermute x16, starting transfers between devices, cross(): lax.ppermute(block, 'expert', [(e, e ^ step) for e in range(expert_count)])  21 us
    ppermute x6, starting transfers between devices, swap(): return lax.ppermute(block, 'sub', [(0, 1), (1, 0)])  2.84 us
  transfers between devices with their start and end apart: 22, of which 11 were waited for; matrix products, arithmetic and copies ran while one was open for 0% of the time, Pallas kernels for 25%

profile of v4, /device:TPU:19, one launch (start us, length us, event | category | flops | bytes accessed | tf_op | source)
XLA Modules:
  0.0 102.6 jit_solution(13902199079676272122)
XLA Ops:
  1.3 1.6 %shard_map.95.refs_0_ = bf16[64,2176]{1,0:T(8,128)(2,1)S(1)} custom-call(s32[1]{0:T(128)S(6)} %copy.11.live_ref, bf16[64,2048]{1,0:T(8,128)(2,1)} %hidden_hbm.1, f32[1,2048]{1,0:T(1,128)} %bitcast.12, bf16[16,2048]{1,0:T(8,128)(2,1)} %bitcast.11, s32[6,64]{1,0:T(8,128)} %bitcast.13), custom_call_target="tpu_custom_call" | custom-call | flops 4194304 | bytes 524288 | tf_op jit(solution)/shard_map/pallas_call | solution.py:253
  3.0 1.3 %collective-permute-start = (bf16[64,2176]{1,0:T(8,128)(2,1)S(1)}, bf16[64,2176]{1,0:T(8,128)(2,1)S(1)}, u32[]{:S(2)}, u32[]{:S(2)}) collective-permute-start(bf16[64,2176]{1,0:T(8,128)(2,1)S(1)} %shard_map.95.refs_0_), channel_id=1, source_target_pairs={{0,2},{2,0},{4,6},{6,4},{8,10},{10,8},{12,14},{14,12},{1,3},{3,1},... | collective-permute-start | bytes 835592 | tf_op jit(solution)/shard_map/ppermute | solution.py:293
  4.3 10.1 %collective-permute-done.3.refs_2_.refs_0_ = bf16[64,2176]{1,0:T(8,128)(2,1)S(1)} collective-permute-done((bf16[64,2176]{1,0:T(8,128)(2,1)S(1)}, bf16[64,2176]{1,0:T(8,128)(2,1)S(1)}, u32[]{:S(2)}, u32[]{:S(2)}) %collective-permute-start.3) | collective-permute-done | bytes 278560 | tf_op jit(solution)/shard_map/ppermute | solution.py:293
  14.4 5.2 %collective-permute-start.7 = (bf16[64,2176]{1,0:T(8,128)(2,1)S(1)}, bf16[64,2176]{1,0:T(8,128)(2,1)S(1)}, u32[]{:S(2)}, u32[]{:S(2)}) collective-permute-start(bf16[64,2176]{1,0:T(8,128)(2,1)S(1)} %collective-permute-done.3.refs_2_.refs_0_), channel_id=1, source_target_pairs={{0,4},{2,6},{4,0},{6,2},{8,12},{10,14},{12,8},{14,10},{1,5},{3,7},... | collective-permute-start | bytes 835592 | tf_op jit(solution)/shard_map/ppermute | solution.py:293
  19.6 1.4 %collective-permute-start.6 = (bf16[64,2176]{1,0:T(8,128)(2,1)S(1)}, bf16[64,2176]{1,0:T(8,128)(2,1)S(1)}, u32[]{:S(2)}, u32[]{:S(2)}) collective-permute-start(bf16[64,2176]{1,0:T(8,128)(2,1)S(1)} %collective-permute-done.refs_1_), channel_id=1, source_target_pairs={{0,4},{2,6},{4,0},{6,2},{8,12},{10,14},{12,8},{14,10},{1,5},{3,7},... | collective-permute-start | bytes 835592 | tf_op jit(solution)/shard_map/ppermute | solution.py:293
  21.1 5.1 %collective-permute-done.7.refs_2_ = bf16[64,2176]{1,0:T(8,128)(2,1)S(1)} collective-permute-done((bf16[64,2176]{1,0:T(8,128)(2,1)S(1)}, bf16[64,2176]{1,0:T(8,128)(2,1)S(1)}, u32[]{:S(2)}, u32[]{:S(2)}) %collective-permute-start.7) | collective-permute-done | bytes 278560 | tf_op jit(solution)/shard_map/ppermute | solution.py:293
  26.1 1.2 %collective-permute-start.8 = (bf16[64,2176]{1,0:T(8,128)(2,1)S(1)}, bf16[64,2176]{1,0:T(8,128)(2,1)S(1)}, u32[]{:S(2)}, u32[]{:S(2)}) collective-permute-start(bf16[64,2176]{1,0:T(8,128)(2,1)S(1)} %collective-permute-done.7.refs_2_), channel_id=1, source_target_pairs={{0,2},{2,0},{4,6},{6,4},{8,10},{10,8},{12,14},{14,12},{1,3},{3,1},... | collective-permute-start | bytes 835592 | tf_op jit(solution)/shard_map/ppermute | solution.py:293
  27.4 4.7 %collective-permute-done.5.refs_0_ = bf16[64,2176]{1,0:T(8,128)(2,1)S(1)} collective-permute-done((bf16[64,2176]{1,0:T(8,128)(2,1)S(1)}, bf16[64,2176]{1,0:T(8,128)(2,1)S(1)}, u32[]{:S(2)}, u32[]{:S(2)}) %collective-permute-start.5) | collective-permute-done | bytes 278560 | tf_op jit(solution)/shard_map/ppermute | solution.py:293
  32.1 6.0 %collective-permute-done.6.refs_1_ = bf16[64,2176]{1,0:T(8,128)(2,1)S(1)} collective-permute-done((bf16[64,2176]{1,0:T(8,128)(2,1)S(1)}, bf16[64,2176]{1,0:T(8,128)(2,1)S(1)}, u32[]{:S(2)}, u32[]{:S(2)}) %collective-permute-start.6) | collective-permute-done | bytes 278560 | tf_op jit(solution)/shard_map/ppermute | solution.py:293
  41.1 4.3 %shard_map.97.up_ref = bf16[2048,2816]{1,0:T(8,128)(2,1)S(1)} custom-call(bf16[2048,2816]{1,0:T(8,128)(2,1)} %bitcast.8), custom_call_target="tpu_custom_call" | custom-call | bytes 11534336 | tf_op jit(solution)/shard_map/pallas_call | solution.py:253
  45.4 3.9 %shard_map.98 = (bf16[1408,2048]{1,0:T(8,128)(2,1)S(1)}, bf16[3,352,2048]{2,1,0:T(8,128)(2,1)S(1)}) custom-call(bf16[1408,2048]{1,0:T(8,128)(2,1)} %bitcast.9, bf16[3,352,2048]{2,1,0:T(8,128)(2,1)} %bitcast.10), custom_call_target="tpu_custom_call" | custom-call | bytes 10092544 | tf_op jit(solution)/shard_map/pallas_call | solution.py:253
  51.0 5.0 %shard_map.103 = (bf16[128,2048]{1,0:T(8,128)(2,1)S(1)}, bf16[128,2048]{1,0:T(8,128)(2,1)S(1)}) custom-call(bf16[144,2048]{1,0:T(8,128)(2,1)S(1)} %get-tuple-element.36.mine_ref, bf16[144,2048]{1,0:T(8,128)(2,1)S(1)} %collective-permute-done.9.peer_ref, bf16[2048,2816]{1,0:T(8,128)(2,1)S(1)} %shard_map.97.up_ref, ...), custom_call_target="tpu_custom_call" | custom-call | flops 4429185024 | bytes 17301504 | tf_op jit(solution)/shard_map/pallas_call | solution.py:253
  56.4 1.9 %shard_map.100 = (f32[128,2048]{1,0:T(8,128)S(1)}, f32[128,2048]{1,0:T(8,128)S(1)}) custom-call(bf16[64,2176]{1,0:T(8,128)(2,1)S(1)} %shard_map.95.refs_0_, bf16[64,2176]{1,0:T(8,128)(2,1)S(1)} %collective-permute-done.refs_1_, bf16[64,2176]{1,0:T(8,128)(2,1)S(1)} %collective-permute-done.3.refs_2_.refs_0_, ...), custom_call_target="tpu_custom_call" | custom-call | flops 1107296256 | bytes 4325376 | tf_op jit(solution)/shard_map/pallas_call | solution.py:253
  58.3 2.6 %shard_map.107 = (bf16[64,2048]{1,0:T(8,128)(2,1)S(1)}, bf16[64,2048]{1,0:T(8,128)(2,1)S(1)}) custom-call(bf16[80,2048]{1,0:T(8,128)(2,1)S(1)} %get-tuple-element.41.mine_ref, bf16[80,2048]{1,0:T(8,128)(2,1)S(1)} %collective-permute-done.12.peer_ref, bf16[2048,2816]{1,0:T(8,128)(2,1)S(1)} %shard_map.97.up_ref, bf16[1408,2048]{1,0:T(8,128)(2,1)S(1)} %get-tuple-element.30.down_ref), custom_call_target="tpu_custom_call" | custom-call | flops 2214592512 | bytes 17301504 | tf_op jit(solution)/shard_map/pallas_call | solution.py:253
  61.2 2.6 %shard_map.99 = (bf16[64,2048]{1,0:T(8,128)(2,1)S(1)}, bf16[64,2048]{1,0:T(8,128)(2,1)S(1)}) custom-call(bf16[80,2048]{1,0:T(8,128)(2,1)S(1)} %get-tuple-element.28.mine_ref, bf16[80,2048]{1,0:T(8,128)(2,1)S(1)} %collective-permute-done.1.peer_ref, bf16[2048,2816]{1,0:T(8,128)(2,1)S(1)} %shard_map.97.up_ref, bf16[1408,2048]{1,0:T(8,128)(2,1)S(1)} %get-tuple-element.30.down_ref), custom_call_target="tpu_custom_call" | custom-call | flops 2214592512 | bytes 17301504 | tf_op jit(solution)/shard_map/pallas_call | solution.py:253
  64.3 2.0 %shard_map.104.refs_6_ = f32[256,2048]{1,0:T(8,128)S(1)} custom-call(bf16[64,2176]{1,0:T(8,128)(2,1)S(1)} %collective-permute-done.5.refs_0_, bf16[64,2176]{1,0:T(8,128)(2,1)S(1)} %collective-permute-done.6.refs_1_, bf16[64,2176]{1,0:T(8,128)(2,1)S(1)} %collective-permute-done.7.refs_2_, bf16[64,2176]{1,0:T(8,128)(2,1)S(1)} %collective-permute-done.8.refs_3_, ...), custom_call_target="tpu_custom_call" | custom-call | flops 1107296256 | bytes 4325376 | tf_op jit(solution)/shard_map/pallas_call | solution.py:253
  67.5 1.5 %collective-permute-start.20 = (bf16[64,2048]{1,0:T(8,128)(2,1)S(1)}, bf16[64,2048]{1,0:T(8,128)(2,1)S(1)}, u32[]{:S(2)}, u32[]{:S(2)}) collective-permute-start(bf16[64,2048]{1,0:T(8,128)(2,1)S(1)} %get-tuple-element.53), channel_id=1, source_target_pairs={{0,4},{2,6},{4,0},{6,2},{8,12},{10,14},{12,8},{14,10},{1,5},{3,7},... | collective-permute-start | bytes 786440 | tf_op jit(solution)/shard_map/ppermute | solution.py:293
  69.4 5.1 %collective-permute-done.14.more_ref = bf16[64,2048]{1,0:T(8,128)(2,1)S(1)} collective-permute-done((bf16[64,2048]{1,0:T(8,128)(2,1)S(1)}, bf16[64,2048]{1,0:T(8,128)(2,1)S(1)}, u32[]{:S(2)}, u32[]{:S(2)}) %collective-permute-start.14) | collective-permute-done | bytes 262176 | tf_op jit(solution)/shard_map/ppermute | solution.py:293
  76.1 1.5 %collective-permute-start.11 = (bf16[64,2048]{1,0:T(8,128)(2,1)S(1)}, bf16[64,2048]{1,0:T(8,128)(2,1)S(1)}, u32[]{:S(2)}, u32[]{:S(2)}) collective-permute-start(bf16[64,2048]{1,0:T(8,128)(2,1)S(1)} %get-tuple-element.40), channel_id=1, source_target_pairs={{0,4},{2,6},{4,0},{6,2},{8,12},{10,14},{12,8},{14,10},{1,5},{3,7},... | collective-permute-start | bytes 786440 | tf_op jit(solution)/shard_map/ppermute | solution.py:293
  78.5 2.9 %collective-permute-start.17 = (bf16[64,1024]{1,0:T(8,128)(2,1)S(1)}, bf16[64,1024]{1,0:T(8,128)(2,1)S(1)}, u32[]{:S(2)}, u32[]{:S(2)}) collective-permute-start(bf16[64,1024]{1,0:T(8,128)(2,1)S(1)} %shard_map.110), channel_id=1, source_target_pairs={{0,12},{2,14},{4,8},{6,10},{8,4},{10,6},{12,0},{14,2},{1,13},{3,15... | collective-permute-start | bytes 393224 | tf_op jit(solution)/shard_map/ppermute | solution.py:293
  81.6 2.3 %collective-permute-start.19 = (bf16[64,1024]{1,0:T(8,128)(2,1)S(1)}, bf16[64,1024]{1,0:T(8,128)(2,1)S(1)}, u32[]{:S(2)}, u32[]{:S(2)}) collective-permute-start(bf16[64,1024]{1,0:T(8,128)(2,1)S(1)} %shard_map.111), channel_id=1, source_target_pairs={{0,12},{2,14},{4,8},{6,10},{8,4},{10,6},{12,0},{14,2},{1,13},{3,15... | collective-permute-start | bytes 393224 | tf_op jit(solution)/shard_map/ppermute | solution.py:293
  85.2 2.2 %collective-permute-done.11.refs_1_ = bf16[64,2048]{1,0:T(8,128)(2,1)S(1)} collective-permute-done((bf16[64,2048]{1,0:T(8,128)(2,1)S(1)}, bf16[64,2048]{1,0:T(8,128)(2,1)S(1)}, u32[]{:S(2)}, u32[]{:S(2)}) %collective-permute-start.11) | collective-permute-done | bytes 262176 | tf_op jit(solution)/shard_map/ppermute | solution.py:293
  87.4 10.4 %collective-permute-done.17.refs_3_ = bf16[64,1024]{1,0:T(8,128)(2,1)S(1)} collective-permute-done((bf16[64,1024]{1,0:T(8,128)(2,1)S(1)}, bf16[64,1024]{1,0:T(8,128)(2,1)S(1)}, u32[]{:S(2)}, u32[]{:S(2)}) %collective-permute-start.17) | collective-permute-done | bytes 131104 | tf_op jit(solution)/shard_map/ppermute | solution.py:293
  97.8 2.8 %collective-permute-done.19.refs_4_ = bf16[64,1024]{1,0:T(8,128)(2,1)S(1)} collective-permute-done((bf16[64,1024]{1,0:T(8,128)(2,1)S(1)}, bf16[64,1024]{1,0:T(8,128)(2,1)S(1)}, u32[]{:S(2)}, u32[]{:S(2)}) %collective-permute-start.19) | collective-permute-done | bytes 131104 | tf_op jit(solution)/shard_map/ppermute | solution.py:293
  (46 shorter events, 12.2 us)
Async XLA Ops:
  2.9 11.5 %collective-permute-start.3 = (bf16[64,2176]{1,0:T(8,128)(2,1)S(1)}, bf16[64,2176]{1,0:T(8,128)(2,1)S(1)}, u32[]{:S(2)}, u32[]{:S(2)}) collective-permute-start(bf16[64,2176]{1,0:T(8,128)(2,1)S(1)} %shard_map.95.refs_0_), channel_id=1, source_target_pairs={{0,8},{2,10},{4,12},{6,14},{8,0},{10,2},{12,4},{14,6},{1,9},{3,11}... | collective-permute-start | bytes 835592 | tf_op jit(solution)/shard_map/ppermute | solution.py:293
  3.0 16.6 %collective-permute-start = (bf16[64,2176]{1,0:T(8,128)(2,1)S(1)}, bf16[64,2176]{1,0:T(8,128)(2,1)S(1)}, u32[]{:S(2)}, u32[]{:S(2)}) collective-permute-start(bf16[64,2176]{1,0:T(8,128)(2,1)S(1)} %shard_map.95.refs_0_), channel_id=1, source_target_pairs={{0,2},{2,0},{4,6},{6,4},{8,10},{10,8},{12,14},{14,12},{1,3},{3,1},... | collective-permute-start | bytes 835592 | tf_op jit(solution)/shard_map/ppermute | solution.py:293
  14.4 11.8 %collective-permute-start.7 = (bf16[64,2176]{1,0:T(8,128)(2,1)S(1)}, bf16[64,2176]{1,0:T(8,128)(2,1)S(1)}, u32[]{:S(2)}, u32[]{:S(2)}) collective-permute-start(bf16[64,2176]{1,0:T(8,128)(2,1)S(1)} %collective-permute-done.3.refs_2_.refs_0_), channel_id=1, source_target_pairs={{0,4},{2,6},{4,0},{6,2},{8,12},{10,14},{12,8},{14,10},{1,5},{3,7},... | collective-permute-start | bytes 835592 | tf_op jit(solution)/shard_map/ppermute | solution.py:293
  19.6 12.5 %collective-permute-start.5 = (bf16[64,2176]{1,0:T(8,128)(2,1)S(1)}, bf16[64,2176]{1,0:T(8,128)(2,1)S(1)}, u32[]{:S(2)}, u32[]{:S(2)}) collective-permute-start(bf16[64,2176]{1,0:T(8,128)(2,1)S(1)} %shard_map.95.refs_0_), channel_id=1, source_target_pairs={{0,4},{2,6},{4,0},{6,2},{8,12},{10,14},{12,8},{14,10},{1,5},{3,7},... | collective-permute-start | bytes 835592 | tf_op jit(solution)/shard_map/ppermute | solution.py:293
  19.6 18.5 %collective-permute-start.6 = (bf16[64,2176]{1,0:T(8,128)(2,1)S(1)}, bf16[64,2176]{1,0:T(8,128)(2,1)S(1)}, u32[]{:S(2)}, u32[]{:S(2)}) collective-permute-start(bf16[64,2176]{1,0:T(8,128)(2,1)S(1)} %collective-permute-done.refs_1_), channel_id=1, source_target_pairs={{0,4},{2,6},{4,0},{6,2},{8,12},{10,14},{12,8},{14,10},{1,5},{3,7},... | collective-permute-start | bytes 835592 | tf_op jit(solution)/shard_map/ppermute | solution.py:293
  26.1 11.9 %collective-permute-start.8 = (bf16[64,2176]{1,0:T(8,128)(2,1)S(1)}, bf16[64,2176]{1,0:T(8,128)(2,1)S(1)}, u32[]{:S(2)}, u32[]{:S(2)}) collective-permute-start(bf16[64,2176]{1,0:T(8,128)(2,1)S(1)} %collective-permute-done.7.refs_2_), channel_id=1, source_target_pairs={{0,2},{2,0},{4,6},{6,4},{8,10},{10,8},{12,14},{14,12},{1,3},{3,1},... | collective-permute-start | bytes 835592 | tf_op jit(solution)/shard_map/ppermute | solution.py:293
  38.8 12.2 %collective-permute-start.9 = (bf16[144,2048]{1,0:T(8,128)(2,1)S(1)}, bf16[144,2048]{1,0:T(8,128)(2,1)S(1)}, u32[]{:S(2)}, u32[]{:S(2)}) collective-permute-start(bf16[144,2048]{1,0:T(8,128)(2,1)S(1)} %get-tuple-element.37), channel_id=1, source_target_pairs={{0,1},{1,0},{2,3},{3,2},{4,5},{5,4},{6,7},{7,6},{8,9},{9,8},{10,11... | collective-permute-start | bytes 1769480 | tf_op jit(solution)/shard_map/ppermute | solution.py:296
  39.9 10.4 %collective-permute-start.4 = (bf16[64,2176]{1,0:T(8,128)(2,1)S(1)}, bf16[64,2176]{1,0:T(8,128)(2,1)S(1)}, u32[]{:S(2)}, u32[]{:S(2)}) collective-permute-start(bf16[64,2176]{1,0:T(8,128)(2,1)S(1)} %collective-permute-done.3.refs_2_.refs_0_), channel_id=1, source_target_pairs={{0,2},{2,0},{4,6},{6,4},{8,10},{10,8},{12,14},{14,12},{1,3},{3,1},... | collective-permute-start | bytes 835592 | tf_op jit(solution)/shard_map/ppermute | solution.py:293
  49.8 11.3 %collective-permute-start.1 = (bf16[80,2048]{1,0:T(8,128)(2,1)S(1)}, bf16[80,2048]{1,0:T(8,128)(2,1)S(1)}, u32[]{:S(2)}, u32[]{:S(2)}) collective-permute-start(bf16[80,2048]{1,0:T(8,128)(2,1)S(1)} %get-tuple-element.29), channel_id=1, source_target_pairs={{0,1},{1,0},{2,3},{3,2},{4,5},{5,4},{6,7},{7,6},{8,9},{9,8},{10,11... | collective-permute-start | bytes 983048 | tf_op jit(solution)/shard_map/ppermute | solution.py:296
  50.7 7.6 %collective-permute-start.12 = (bf16[80,2048]{1,0:T(8,128)(2,1)S(1)}, bf16[80,2048]{1,0:T(8,128)(2,1)S(1)}, u32[]{:S(2)}, u32[]{:S(2)}) collective-permute-start(bf16[80,2048]{1,0:T(8,128)(2,1)S(1)} %get-tuple-element.42), channel_id=1, source_target_pairs={{0,1},{1,0},{2,3},{3,2},{4,5},{5,4},{6,7},{7,6},{8,9},{9,8},{10,11... | collective-permute-start | bytes 983048 | tf_op jit(solution)/shard_map/ppermute | solution.py:296
  56.0 11.0 %collective-permute-start.10 = (bf16[128,2048]{1,0:T(8,128)(2,1)S(1)}, bf16[128,2048]{1,0:T(8,128)(2,1)S(1)}, u32[]{:S(2)}, u32[]{:S(2)}) collective-permute-start(bf16[128,2048]{1,0:T(8,128)(2,1)S(1)} %get-tuple-element.39), channel_id=1, source_target_pairs={{0,1},{1,0},{2,3},{3,2},{4,5},{5,4},{6,7},{7,6},{8,9},{9,8},{10,11... | collective-permute-start | bytes 1572872 | tf_op jit(solution)/shard_map/ppermute | solution.py:296
  61.0 5.3 %collective-permute-start.13 = (bf16[64,2048]{1,0:T(8,128)(2,1)S(1)}, bf16[64,2048]{1,0:T(8,128)(2,1)S(1)}, u32[]{:S(2)}, u32[]{:S(2)}) collective-permute-start(bf16[64,2048]{1,0:T(8,128)(2,1)S(1)} %get-tuple-element.44), channel_id=1, source_target_pairs={{0,1},{1,0},{2,3},{3,2},{4,5},{5,4},{6,7},{7,6},{8,9},{9,8},{10,11... | collective-permute-start | bytes 786440 | tf_op jit(solution)/shard_map/ppermute | solution.py:296
  63.8 5.2 %collective-permute-start.2 = (bf16[64,2048]{1,0:T(8,128)(2,1)S(1)}, bf16[64,2048]{1,0:T(8,128)(2,1)S(1)}, u32[]{:S(2)}, u32[]{:S(2)}) collective-permute-start(bf16[64,2048]{1,0:T(8,128)(2,1)S(1)} %get-tuple-element.32), channel_id=1, source_target_pairs={{0,1},{1,0},{2,3},{3,2},{4,5},{5,4},{6,7},{7,6},{8,9},{9,8},{10,11... | collective-permute-start | bytes 786440 | tf_op jit(solution)/shard_map/ppermute | solution.py:296
  66.7 7.8 %collective-permute-start.14 = (bf16[64,2048]{1,0:T(8,128)(2,1)S(1)}, bf16[64,2048]{1,0:T(8,128)(2,1)S(1)}, u32[]{:S(2)}, u32[]{:S(2)}) collective-permute-start(bf16[64,2048]{1,0:T(8,128)(2,1)S(1)} %get-tuple-element.47), channel_id=1, source_target_pairs={{0,2},{2,0},{4,6},{6,4},{8,10},{10,8},{12,14},{14,12},{1,3},{3,1},... | collective-permute-start | bytes 786440 | tf_op jit(solution)/shard_map/ppermute | solution.py:293
  67.5 10.1 %collective-permute-start.20 = (bf16[64,2048]{1,0:T(8,128)(2,1)S(1)}, bf16[64,2048]{1,0:T(8,128)(2,1)S(1)}, u32[]{:S(2)}, u32[]{:S(2)}) collective-permute-start(bf16[64,2048]{1,0:T(8,128)(2,1)S(1)} %get-tuple-element.53), channel_id=1, source_target_pairs={{0,4},{2,6},{4,0},{6,2},{8,12},{10,14},{12,8},{14,10},{1,5},{3,7},... | collective-permute-start | bytes 786440 | tf_op jit(solution)/shard_map/ppermute | solution.py:293
  74.5 10.7 %collective-permute-start.15 = (bf16[64,2048]{1,0:T(8,128)(2,1)S(1)}, bf16[64,2048]{1,0:T(8,128)(2,1)S(1)}, u32[]{:S(2)}, u32[]{:S(2)}) collective-permute-start(bf16[64,2048]{1,0:T(8,128)(2,1)S(1)} %shard_map.109), channel_id=1, source_target_pairs={{0,8},{2,10},{4,12},{6,14},{8,0},{10,2},{12,4},{14,6},{1,9},{3,11}... | collective-permute-start | bytes 786440 | tf_op jit(solution)/shard_map/ppermute | solution.py:293
  74.6 3.9 %collective-permute-start.16 = (bf16[64,1024]{1,0:T(8,128)(2,1)S(1)}, bf16[64,1024]{1,0:T(8,128)(2,1)S(1)}, u32[]{:S(2)}, u32[]{:S(2)}) collective-permute-start(bf16[64,1024]{1,0:T(8,128)(2,1)S(1)} %get-tuple-element.49), channel_id=1, source_target_pairs={{0,2},{2,0},{4,6},{6,4},{8,10},{10,8},{12,14},{14,12},{1,3},{3,1},... | collective-permute-start | bytes 393224 | tf_op jit(solution)/shard_map/ppermute | solution.py:293
  74.9 6.6 %collective-permute-start.18 = (bf16[64,1024]{1,0:T(8,128)(2,1)S(1)}, bf16[64,1024]{1,0:T(8,128)(2,1)S(1)}, u32[]{:S(2)}, u32[]{:S(2)}) collective-permute-start(bf16[64,1024]{1,0:T(8,128)(2,1)S(1)} %get-tuple-element.51), channel_id=1, source_target_pairs={{0,2},{2,0},{4,6},{6,4},{8,10},{10,8},{12,14},{14,12},{1,3},{3,1},... | collective-permute-start | bytes 393224 | tf_op jit(solution)/shard_map/ppermute | solution.py:293
  76.1 11.3 %collective-permute-start.11 = (bf16[64,2048]{1,0:T(8,128)(2,1)S(1)}, bf16[64,2048]{1,0:T(8,128)(2,1)S(1)}, u32[]{:S(2)}, u32[]{:S(2)}) collective-permute-start(bf16[64,2048]{1,0:T(8,128)(2,1)S(1)} %get-tuple-element.40), channel_id=1, source_target_pairs={{0,4},{2,6},{4,0},{6,2},{8,12},{10,14},{12,8},{14,10},{1,5},{3,7},... | collective-permute-start | bytes 786440 | tf_op jit(solution)/shard_map/ppermute | solution.py:293
  77.7 23.0 %collective-permute-start.21 = (bf16[64,2048]{1,0:T(8,128)(2,1)S(1)}, bf16[64,2048]{1,0:T(8,128)(2,1)S(1)}, u32[]{:S(2)}, u32[]{:S(2)}) collective-permute-start(bf16[64,2048]{1,0:T(8,128)(2,1)S(1)} %shard_map.112), channel_id=1, source_target_pairs={{0,2},{2,0},{4,6},{6,4},{8,10},{10,8},{12,14},{14,12},{1,3},{3,1},... | collective-permute-start | bytes 786440 | tf_op jit(solution)/shard_map/ppermute | solution.py:293
  78.5 19.3 %collective-permute-start.17 = (bf16[64,1024]{1,0:T(8,128)(2,1)S(1)}, bf16[64,1024]{1,0:T(8,128)(2,1)S(1)}, u32[]{:S(2)}, u32[]{:S(2)}) collective-permute-start(bf16[64,1024]{1,0:T(8,128)(2,1)S(1)} %shard_map.110), channel_id=1, source_target_pairs={{0,12},{2,14},{4,8},{6,10},{8,4},{10,6},{12,0},{14,2},{1,13},{3,15... | collective-permute-start | bytes 393224 | tf_op jit(solution)/shard_map/ppermute | solution.py:293
  81.6 19.1 %collective-permute-start.19 = (bf16[64,1024]{1,0:T(8,128)(2,1)S(1)}, bf16[64,1024]{1,0:T(8,128)(2,1)S(1)}, u32[]{:S(2)}, u32[]{:S(2)}) collective-permute-start(bf16[64,1024]{1,0:T(8,128)(2,1)S(1)} %shard_map.111), channel_id=1, source_target_pairs={{0,12},{2,14},{4,8},{6,10},{8,4},{10,6},{12,0},{14,2},{1,13},{3,15... | collective-permute-start | bytes 393224 | tf_op jit(solution)/shard_map/ppermute | solution.py:293
